TPU v7x, 256 devices: a whole 4x4x8 slice. The times are simulated.
256 devices in a mesh: ctx: 16 (over y, x_hi, core), head: 8 (over z), dp: 2 (over x_lo).
Axes of the slice: x: 4 (x_hi: 2, x_lo: 2; x = x_hi * 2 + x_lo), y: 4, z: 8, core: 2. Of those that a mesh axis runs over, the one named last changes fastest.
Arguments:
- queries: bfloat16 [8192, 8192], P(('dp', 'ctx', 'head')), parts along dimension 0, may hold values from -100 to 100, as said below
- unscaled_key_rows: bfloat16 [8192, 1024], P(('dp', 'ctx', 'head')), parts along dimension 0, may hold values from -4 to 4
- unscaled_value_rows: bfloat16 [8192, 1024], P(('dp', 'ctx', 'head')), parts along dimension 0, may hold values from -12 to 12
- key_block_scale: float32 [64, 8], P('dp', 'head'), parts along dimension 0, may hold values from 0.8 to 1.6
- value_block_scale: float32 [64, 8], P('dp', 'head'), parts along dimension 0, may hold values from 0.5 to 2
- span_order: int32 [32], replicated, may hold values from 0 to 31, each once
- block_keep: int32 [32, 32], replicated, may hold values 0 or 1
Outputs:
- attended: bfloat16 [8192, 8192], P(('dp', 'ctx', 'head')), parts along dimension 0
- row_check: float32 [8192, 64], P(('dp', 'ctx', 'head')), parts along dimension 0
There are 2 independent parts, one for each index of `dp`. A program takes and returns all parts, laid end to end along the dimension named above; an argument that names none is the same for every part. Nothing has to cross between parts.
Inputs may be any that keep to these rules, and one draw needn't show every extreme that they name: `queries`: queries of one head and token.
All inputs are finite; a program needn't handle non-finite values.
Results may differ from a plain program's by a relative error of at most 0.004.
Values may be sent and summed in bfloat16 or wider, within the bound.
A program may use at most 64 MiB of HBM per device.

v0:
```python
import math

import jax
import jax.numpy as jnp
from jax import lax
from jax.sharding import PartitionSpec as P

HEAD_WIDTH = 128
SPAN = 128


def passed_along(block, axis, distance):
    devices = range(lax.axis_size(axis))
    route = [((i - distance) % len(devices), i) for i in devices]
    return lax.ppermute(block, axis, route)


def local(
    queries,
    unscaled_key_rows,
    unscaled_value_rows,
    key_block_scale,
    value_block_scale,
    span_order,
    block_keep,
):
    head_queries, head_keys, head_values = (
        lax.all_to_all(queries, "head", split_axis=1, concat_axis=0, tiled=True),
        lax.all_to_all(unscaled_key_rows, "head", split_axis=1, concat_axis=0, tiled=True),
        lax.all_to_all(unscaled_value_rows, "head", split_axis=1, concat_axis=0, tiled=True),
    )
    cycle_size = lax.axis_size("ctx")
    cycle_place = lax.axis_index("ctx")
    local_rows = head_queries.shape[0]
    kv_local = head_keys.shape[1] // HEAD_WIDTH
    query_group_count = head_queries.shape[1] // HEAD_WIDTH // kv_local
    inverse_root = 1.0 / math.sqrt(HEAD_WIDTH)
    query_block = head_queries.reshape(local_rows, kv_local, query_group_count, HEAD_WIDTH)
    first_own = 2 * cycle_place
    row_index = jnp.arange(local_rows, dtype=jnp.int32)
    own_order = lax.dynamic_slice_in_dim(span_order, first_own, 2, 0)
    query_position = jnp.repeat(own_order, SPAN) * SPAN + row_index % SPAN
    own_keep = lax.dynamic_slice_in_dim(block_keep, first_own, 2, 0)
    own_spans = first_own + jnp.arange(2, dtype=jnp.int32)
    column_index = jnp.arange(SPAN, dtype=jnp.int32)

    def pair_allowed(span_number):
        keep_column = lax.dynamic_index_in_dim(own_keep, span_number, 1, keepdims=False)
        return (keep_column > 0) | (own_spans == span_number)

    def absorb(state, span_keys, span_values, span_number):
        highest, totals, mixed, checks = state
        key_order = lax.dynamic_index_in_dim(span_order, span_number, 0, keepdims=False)
        key_position = key_order * SPAN + column_index
        allowed = jnp.repeat(pair_allowed(span_number), SPAN)[:, None] & (
            query_position[:, None] >= key_position[None, :]
        )
        key_factor = (
            lax.dynamic_index_in_dim(key_block_scale, span_number, 0, keepdims=False) * inverse_root
        )
        value_factor = lax.dynamic_index_in_dim(value_block_scale, span_number, 0, keepdims=False)
        key_head_count = span_keys.reshape(SPAN, kv_local, HEAD_WIDTH)
        value_head_count = span_values.reshape(SPAN, kv_local, HEAD_WIDTH)
        scores = jnp.einsum(
            "tkgd,skd->kgts", query_block, key_head_count, preferred_element_type=jnp.float32
        )
        scores = scores * key_factor[:, None, None, None]
        masked = jnp.where(allowed, scores, jnp.float32(-1e30))
        new_high = jnp.maximum(highest, jnp.max(masked, axis=3))
        weights = jnp.where(allowed, jnp.exp(masked - new_high[..., None]), jnp.float32(0.0))
        fading = jnp.exp(highest - new_high)
        rounded = weights.astype(jnp.bfloat16)
        value_sum = jnp.einsum(
            "kgts,skd->kgtd", rounded, value_head_count, preferred_element_type=jnp.float32
        )
        value_check = (
            value_factor[None, :]
            * jnp.sum(value_head_count.astype(jnp.float32), axis=2)
            * inverse_root
        )
        check_sum = jnp.einsum(
            "kgts,sk->kgt",
            rounded.astype(jnp.float32),
            value_check,
            precision=lax.Precision.HIGHEST,
        )
        new_totals = totals * fading + jnp.sum(weights, axis=3)
        new_mixed = mixed * fading[..., None] + value_factor[:, None, None, None] * value_sum
        return (new_high, new_totals, new_mixed, checks * fading + check_sum)

    def visit(state, span_keys, span_values, span_number):
        return absorb(state, span_keys, span_values, span_number)

    def visit_pair(state, pair_keys, pair_values, source):
        for member in range(2):
            span_keys = pair_keys[member * SPAN : (member + 1) * SPAN]
            span_values = pair_values[member * SPAN : (member + 1) * SPAN]
            state = visit(state, span_keys, span_values, 2 * source + member)
        return state

    initial = (
        jnp.full((kv_local, query_group_count, local_rows), -1e30, jnp.float32),
        jnp.zeros((kv_local, query_group_count, local_rows), jnp.float32),
        jnp.zeros((kv_local, query_group_count, local_rows, HEAD_WIDTH), jnp.float32),
        jnp.zeros((kv_local, query_group_count, local_rows), jnp.float32),
    )
    state = visit_pair(initial, head_keys, head_values, cycle_place)

    def cycle_turn(turn_index, carried):
        state, moving_keys, moving_values = carried
        moving_keys, moving_values = passed_along((moving_keys, moving_values), "ctx", 1)
        source = (cycle_place - turn_index) % cycle_size
        return (visit_pair(state, moving_keys, moving_values, source), moving_keys, moving_values)

    state = lax.fori_loop(1, cycle_size, cycle_turn, (state, head_keys, head_values))[0]
    highest, totals, mixed, checks = state
    output = (mixed / totals[..., None]).astype(jnp.bfloat16)
    output = jnp.transpose(output, (2, 0, 1, 3)).reshape(
        local_rows, kv_local * query_group_count * HEAD_WIDTH
    )
    check_out = jnp.transpose(checks / totals, (2, 0, 1)).reshape(
        local_rows, kv_local * query_group_count
    )
    attended = lax.all_to_all(output, "head", split_axis=0, concat_axis=1, tiled=True)
    row_check = lax.all_to_all(check_out, "head", split_axis=0, concat_axis=1, tiled=True)
    return (attended, row_check)


def solution(mesh):
    placed = (
        P(("dp", "ctx", "head"), None),
        P(("dp", "ctx", "head"), None),
        P(("dp", "ctx", "head"), None),
        P("dp", "head"),
        P("dp", "head"),
        P(),
        P(),
    )
    return jax.shard_map(
        local,
        mesh=mesh,
        in_specs=placed,
        out_specs=(P(("dp", "ctx", "head"), None), P(("dp", "ctx", "head"), None)),
        check_vma=False,
    )
```

profile of v0, /device:TPU:30, one launch (start us, length us, event | category | flops | bytes accessed | tf_op | source)
XLA Modules:
  0.0 297.4 jit_solution(14692853476416949173)
XLA Ops:
  2.1 8.6 %all-to-all-start = ((bf16[32,8,128]{2,0,1:T(8,128)(2,1)}), bf16[32,8,128]{2,0,1:T(8,128)(2,1)S(1)}, u32[]{:S(2)}, u32[]{:S(2)}) async-start(bf16[32,8,128]{2,0,1:T(8,128)(2,1)} %copy_bitcast_fusion.2), calls=%async_computation | async-start | bytes 131072 | tf_op jit(solution)/shard_map/all_to_all | solution.py:29
  14.0 1.9 copy.81
  19.8 7.2 %all-to-all-start.2 = ((bf16[32,8,128]{2,0,1:T(8,128)(2,1)}), bf16[32,8,128]{2,0,1:T(8,128)(2,1)S(1)}, u32[]{:S(2)}, u32[]{:S(2)}) async-start(bf16[32,8,128]{2,0,1:T(8,128)(2,1)} %copy_bitcast_fusion.1), calls=%async_computation.2 | async-start | bytes 131072 | tf_op jit(solution)/shard_map/all_to_all | solution.py:30
  27.2 8.3 %all-to-all-done.2 = bf16[32,8,128]{2,0,1:T(8,128)(2,1)S(1)} async-done(((bf16[32,8,128]{2,0,1:T(8,128)(2,1)}), bf16[32,8,128]{2,0,1:T(8,128)(2,1)S(1)}, u32[]{:S(2)}, u32[]{:S(2)}) %all-to-all-start.2) | async-done | bytes 65568 | tf_op jit(solution)/shard_map/all_to_all | solution.py:30
  35.4 3.5 %all-to-all-start.1 = ((bf16[32,8,1024]{2,0,1:T(8,128)(2,1)}), bf16[32,8,1024]{2,0,1:T(8,128)(2,1)S(1)}, u32[]{:S(2)}, u32[]{:S(2)}) async-start(bf16[32,8,1024]{2,0,1:T(8,128)(2,1)} %bitcast.254), calls=%async_computation.1 | async-start | bytes 1048576 | tf_op jit(solution)/shard_map/all_to_all | solution.py:28
  40.5 14.1 %all-to-all-done.1 = bf16[32,8,1024]{2,0,1:T(8,128)(2,1)S(1)} async-done(((bf16[32,8,1024]{2,0,1:T(8,128)(2,1)}), bf16[32,8,1024]{2,0,1:T(8,128)(2,1)S(1)}, u32[]{:S(2)}, u32[]{:S(2)}) %all-to-all-start.1) | async-done | bytes 524320 | tf_op jit(solution)/shard_map/all_to_all | solution.py:28
  56.8 1.6 fusion.57
  59.3 205.1 %while.27 = (s32[]{:T(128)}, f32[1,8,256]{2,1,0:T(8,128)S(1)}, f32[1,8,256]{2,1,0:T(8,128)S(1)}, f32[1,8,256,128]{3,2,1,0:T(8,128)S(1)}, f32[1,8,256]{2,1,0:T(8,...) while((s32[]{:T(128)}, f32[1,8,256]{2,1,0:T(8,128)S(1)}, ...), condition=%wide.region_13.14_spmd.clone.clone, body=%wide.region_6.13_spmd.clone.clone.sunk | while | flops 282812704 | bytes 15253182 | solution.py:115
  59.4 1.2 collective-permute-start.1
  65.8 1.1 fusion.138
  69.3 1.9 fusion.142
  71.4 3.0 %collective-permute-start.1 = (bf16[256,128]{1,0:T(8,128)(2,1)S(1)}, bf16[256,128]{1,0:T(8,128)(2,1)S(1)}, u32[]{:S(2)}, u32[]{:S(2)}) collective-permute-start(bf16[256,128]{1,0:T(8,128)(2,1)S(1)} %get-tuple-element.753), channel_id=1, source_target_pairs={{240,0},{0,16},{16,32},{32,48},{48,64},{64,80},{80,96},{96,112},{1... | collective-permute-start | bytes 196616 | tf_op jit(solution)/shard_map/while/body/eval_jaxpr/ppermute | solution.py:15
  79.6 1.1 fusion.138
  83.1 1.9 fusion.142
  85.2 3.0 %collective-permute-start.1 = (bf16[256,128]{1,0:T(8,128)(2,1)S(1)}, bf16[256,128]{1,0:T(8,128)(2,1)S(1)}, u32[]{:S(2)}, u32[]{:S(2)}) collective-permute-start(bf16[256,128]{1,0:T(8,128)(2,1)S(1)} %get-tuple-element.753), channel_id=1, source_target_pairs={{240,0},{0,16},{16,32},{32,48},{48,64},{64,80},{80,96},{96,112},{1... | collective-permute-start | bytes 196616 | tf_op jit(solution)/shard_map/while/body/eval_jaxpr/ppermute | solution.py:15
  93.4 1.1 fusion.138
  96.9 1.9 fusion.142
  99.0 3.0 %collective-permute-start.1 = (bf16[256,128]{1,0:T(8,128)(2,1)S(1)}, bf16[256,128]{1,0:T(8,128)(2,1)S(1)}, u32[]{:S(2)}, u32[]{:S(2)}) collective-permute-start(bf16[256,128]{1,0:T(8,128)(2,1)S(1)} %get-tuple-element.753), channel_id=1, source_target_pairs={{240,0},{0,16},{16,32},{32,48},{48,64},{64,80},{80,96},{96,112},{1... | collective-permute-start | bytes 196616 | tf_op jit(solution)/shard_map/while/body/eval_jaxpr/ppermute | solution.py:15
  110.7 1.9 fusion.142
  112.8 3.0 %collective-permute-start.1 = (bf16[256,128]{1,0:T(8,128)(2,1)S(1)}, bf16[256,128]{1,0:T(8,128)(2,1)S(1)}, u32[]{:S(2)}, u32[]{:S(2)}) collective-permute-start(bf16[256,128]{1,0:T(8,128)(2,1)S(1)} %get-tuple-element.753), channel_id=1, source_target_pairs={{240,0},{0,16},{16,32},{32,48},{48,64},{64,80},{80,96},{96,112},{1... | collective-permute-start | bytes 196616 | tf_op jit(solution)/shard_map/while/body/eval_jaxpr/ppermute | solution.py:15
  124.5 1.9 fusion.142
  126.6 3.0 %collective-permute-start.1 = (bf16[256,128]{1,0:T(8,128)(2,1)S(1)}, bf16[256,128]{1,0:T(8,128)(2,1)S(1)}, u32[]{:S(2)}, u32[]{:S(2)}) collective-permute-start(bf16[256,128]{1,0:T(8,128)(2,1)S(1)} %get-tuple-element.753), channel_id=1, source_target_pairs={{240,0},{0,16},{16,32},{32,48},{48,64},{64,80},{80,96},{96,112},{1... | collective-permute-start | bytes 196616 | tf_op jit(solution)/shard_map/while/body/eval_jaxpr/ppermute | solution.py:15
  134.8 1.1 fusion.138
  138.3 1.9 fusion.142
  140.4 3.0 %collective-permute-start.1 = (bf16[256,128]{1,0:T(8,128)(2,1)S(1)}, bf16[256,128]{1,0:T(8,128)(2,1)S(1)}, u32[]{:S(2)}, u32[]{:S(2)}) collective-permute-start(bf16[256,128]{1,0:T(8,128)(2,1)S(1)} %get-tuple-element.753), channel_id=1, source_target_pairs={{240,0},{0,16},{16,32},{32,48},{48,64},{64,80},{80,96},{96,112},{1... | collective-permute-start | bytes 196616 | tf_op jit(solution)/shard_map/while/body/eval_jaxpr/ppermute | solution.py:15
  152.1 1.9 fusion.142
  154.2 3.0 %collective-permute-start.1 = (bf16[256,128]{1,0:T(8,128)(2,1)S(1)}, bf16[256,128]{1,0:T(8,128)(2,1)S(1)}, u32[]{:S(2)}, u32[]{:S(2)}) collective-permute-start(bf16[256,128]{1,0:T(8,128)(2,1)S(1)} %get-tuple-element.753), channel_id=1, source_target_pairs={{240,0},{0,16},{16,32},{32,48},{48,64},{64,80},{80,96},{96,112},{1... | collective-permute-start | bytes 196616 | tf_op jit(solution)/shard_map/while/body/eval_jaxpr/ppermute | solution.py:15
  165.9 1.9 fusion.142
  168.0 3.0 %collective-permute-start.1 = (bf16[256,128]{1,0:T(8,128)(2,1)S(1)}, bf16[256,128]{1,0:T(8,128)(2,1)S(1)}, u32[]{:S(2)}, u32[]{:S(2)}) collective-permute-start(bf16[256,128]{1,0:T(8,128)(2,1)S(1)} %get-tuple-element.753), channel_id=1, source_target_pairs={{240,0},{0,16},{16,32},{32,48},{48,64},{64,80},{80,96},{96,112},{1... | collective-permute-start | bytes 196616 | tf_op jit(solution)/shard_map/while/body/eval_jaxpr/ppermute | solution.py:15
  176.2 1.1 fusion.138
  179.7 1.9 fusion.142
  181.8 3.0 %collective-permute-start.1 = (bf16[256,128]{1,0:T(8,128)(2,1)S(1)}, bf16[256,128]{1,0:T(8,128)(2,1)S(1)}, u32[]{:S(2)}, u32[]{:S(2)}) collective-permute-start(bf16[256,128]{1,0:T(8,128)(2,1)S(1)} %get-tuple-element.753), channel_id=1, source_target_pairs={{240,0},{0,16},{16,32},{32,48},{48,64},{64,80},{80,96},{96,112},{1... | collective-permute-start | bytes 196616 | tf_op jit(solution)/shard_map/while/body/eval_jaxpr/ppermute | solution.py:15
  190.0 1.1 fusion.138
  193.5 1.9 fusion.142
  195.6 3.0 %collective-permute-start.1 = (bf16[256,128]{1,0:T(8,128)(2,1)S(1)}, bf16[256,128]{1,0:T(8,128)(2,1)S(1)}, u32[]{:S(2)}, u32[]{:S(2)}) collective-permute-start(bf16[256,128]{1,0:T(8,128)(2,1)S(1)} %get-tuple-element.753), channel_id=1, source_target_pairs={{240,0},{0,16},{16,32},{32,48},{48,64},{64,80},{80,96},{96,112},{1... | collective-permute-start | bytes 196616 | tf_op jit(solution)/shard_map/while/body/eval_jaxpr/ppermute | solution.py:15
  207.3 1.9 fusion.142
  209.4 3.0 %collective-permute-start.1 = (bf16[256,128]{1,0:T(8,128)(2,1)S(1)}, bf16[256,128]{1,0:T(8,128)(2,1)S(1)}, u32[]{:S(2)}, u32[]{:S(2)}) collective-permute-start(bf16[256,128]{1,0:T(8,128)(2,1)S(1)} %get-tuple-element.753), channel_id=1, source_target_pairs={{240,0},{0,16},{16,32},{32,48},{48,64},{64,80},{80,96},{96,112},{1... | collective-permute-start | bytes 196616 | tf_op jit(solution)/shard_map/while/body/eval_jaxpr/ppermute | solution.py:15
  221.1 1.9 fusion.142
  223.2 3.0 %collective-permute-start.1 = (bf16[256,128]{1,0:T(8,128)(2,1)S(1)}, bf16[256,128]{1,0:T(8,128)(2,1)S(1)}, u32[]{:S(2)}, u32[]{:S(2)}) collective-permute-start(bf16[256,128]{1,0:T(8,128)(2,1)S(1)} %get-tuple-element.753), channel_id=1, source_target_pairs={{240,0},{0,16},{16,32},{32,48},{48,64},{64,80},{80,96},{96,112},{1... | collective-permute-start | bytes 196616 | tf_op jit(solution)/shard_map/while/body/eval_jaxpr/ppermute | solution.py:15
  234.9 1.9 fusion.142
  237.0 3.0 %collective-permute-start.1 = (bf16[256,128]{1,0:T(8,128)(2,1)S(1)}, bf16[256,128]{1,0:T(8,128)(2,1)S(1)}, u32[]{:S(2)}, u32[]{:S(2)}) collective-permute-start(bf16[256,128]{1,0:T(8,128)(2,1)S(1)} %get-tuple-element.753), channel_id=1, source_target_pairs={{240,0},{0,16},{16,32},{32,48},{48,64},{64,80},{80,96},{96,112},{1... | collective-permute-start | bytes 196616 | tf_op jit(solution)/shard_map/while/body/eval_jaxpr/ppermute | solution.py:15
  248.7 1.9 fusion.142
  250.8 3.0 %collective-permute-start.1 = (bf16[256,128]{1,0:T(8,128)(2,1)S(1)}, bf16[256,128]{1,0:T(8,128)(2,1)S(1)}, u32[]{:S(2)}, u32[]{:S(2)}) collective-permute-start(bf16[256,128]{1,0:T(8,128)(2,1)S(1)} %get-tuple-element.753), channel_id=1, source_target_pairs={{240,0},{0,16},{16,32},{32,48},{48,64},{64,80},{80,96},{96,112},{1... | collective-permute-start | bytes 196616 | tf_op jit(solution)/shard_map/while/body/eval_jaxpr/ppermute | solution.py:15
  262.5 1.9 fusion.142
  265.2 3.3 %all-to-all-start.4 = ((f32[8,1,256]{2,1,0:T(1,128)}), f32[8,1,256]{2,1,0:T(1,128)S(1)}, u32[]{:S(2)}, u32[]{:S(2)}) async-start(f32[8,1,256]{2,1,0:T(1,128)} %reshape.596), calls=%async_computation.4 | async-start | bytes 16384 | tf_op jit(solution)/shard_map/all_to_all | solution.py:125
  270.3 6.0 %all-to-all-done.4 = f32[8,1,256]{2,1,0:T(1,128)S(1)} async-done(((f32[8,1,256]{2,1,0:T(1,128)}), f32[8,1,256]{2,1,0:T(1,128)S(1)}, u32[]{:S(2)}, u32[]{:S(2)}) %all-to-all-start.4) | async-done | bytes 8224 | tf_op jit(solution)/shard_map/all_to_all | solution.py:125
  276.2 3.5 %all-to-all-start.3 = ((bf16[8,32,1024]{2,1,0:T(8,128)(2,1)}), bf16[8,32,1024]{2,1,0:T(8,128)(2,1)S(1)}, u32[]{:S(2)}, u32[]{:S(2)}) async-start(bf16[8,32,1024]{2,1,0:T(8,128)(2,1)} %all_to_all.79), calls=%async_computation.3 | async-start | bytes 1048576 | tf_op jit(solution)/shard_map/all_to_all | solution.py:124
  281.7 14.8 %all-to-all-done.3 = bf16[8,32,1024]{2,1,0:T(8,128)(2,1)S(1)} async-done(((bf16[8,32,1024]{2,1,0:T(8,128)(2,1)}), bf16[8,32,1024]{2,1,0:T(8,128)(2,1)S(1)}, u32[]{:S(2)}, u32[]{:S(2)}) %all-to-all-start.3) | async-done | bytes 524320 | tf_op jit(solution)/shard_map/all_to_all | solution.py:124
  (411 shorter events, 102.2 us)
Async XLA Ops:
  0.6 0.8 copy-start
  2.1 10.5 %copy-start.4 = (bf16[32,1024]{1,0:T(8,128)(2,1)S(1)}, bf16[32,1024]{1,0:T(8,128)(2,1)}, u32[]{:S(2)}) copy-start(bf16[32,1024]{1,0:T(8,128)(2,1)} %param.11) | copy-start | bytes 196612
  2.1 17.7 %all-to-all-start = ((bf16[32,8,128]{2,0,1:T(8,128)(2,1)}), bf16[32,8,128]{2,0,1:T(8,128)(2,1)S(1)}, u32[]{:S(2)}, u32[]{:S(2)}) async-start(bf16[32,8,128]{2,0,1:T(8,128)(2,1)} %copy_bitcast_fusion.2), calls=%async_computation | async-start | bytes 131072 | tf_op jit(solution)/shard_map/all_to_all | solution.py:29
  10.7 0.7 copy-start.3
  17.1 0.7 copy-start.1
  17.1 0.7 copy-start.2
  19.8 15.6 %all-to-all-start.2 = ((bf16[32,8,128]{2,0,1:T(8,128)(2,1)}), bf16[32,8,128]{2,0,1:T(8,128)(2,1)S(1)}, u32[]{:S(2)}, u32[]{:S(2)}) async-start(bf16[32,8,128]{2,0,1:T(8,128)(2,1)} %copy_bitcast_fusion.1), calls=%async_computation.2 | async-start | bytes 131072 | tf_op jit(solution)/shard_map/all_to_all | solution.py:30
  35.4 19.2 %all-to-all-start.1 = ((bf16[32,8,1024]{2,0,1:T(8,128)(2,1)}), bf16[32,8,1024]{2,0,1:T(8,128)(2,1)S(1)}, u32[]{:S(2)}, u32[]{:S(2)}) async-start(bf16[32,8,1024]{2,0,1:T(8,128)(2,1)} %bitcast.254), calls=%async_computation.1 | async-start | bytes 1048576 | tf_op jit(solution)/shard_map/all_to_all | solution.py:28
  59.3 5.5 %collective-permute-start = (bf16[256,128]{1,0:T(8,128)(2,1)S(1)}, bf16[256,128]{1,0:T(8,128)(2,1)S(1)}, u32[]{:S(2)}, u32[]{:S(2)}) collective-permute-start(bf16[256,128]{1,0:T(8,128)(2,1)S(1)} %get-tuple-element.752), channel_id=1, source_target_pairs={{240,0},{0,16},{16,32},{32,48},{48,64},{64,80},{80,96},{96,112},{1... | collective-permute-start | bytes 196616 | tf_op jit(solution)/shard_map/while/body/eval_jaxpr/ppermute | solution.py:15
  59.4 6.2 %collective-permute-start.1 = (bf16[256,128]{1,0:T(8,128)(2,1)S(1)}, bf16[256,128]{1,0:T(8,128)(2,1)S(1)}, u32[]{:S(2)}, u32[]{:S(2)}) collective-permute-start(bf16[256,128]{1,0:T(8,128)(2,1)S(1)} %get-tuple-element.753), channel_id=1, source_target_pairs={{240,0},{0,16},{16,32},{32,48},{48,64},{64,80},{80,96},{96,112},{1... | collective-permute-start | bytes 196616 | tf_op jit(solution)/shard_map/while/body/eval_jaxpr/ppermute | solution.py:15
  71.2 7.4 %collective-permute-start = (bf16[256,128]{1,0:T(8,128)(2,1)S(1)}, bf16[256,128]{1,0:T(8,128)(2,1)S(1)}, u32[]{:S(2)}, u32[]{:S(2)}) collective-permute-start(bf16[256,128]{1,0:T(8,128)(2,1)S(1)} %get-tuple-element.752), channel_id=1, source_target_pairs={{240,0},{0,16},{16,32},{32,48},{48,64},{64,80},{80,96},{96,112},{1... | collective-permute-start | bytes 196616 | tf_op jit(solution)/shard_map/while/body/eval_jaxpr/ppermute | solution.py:15
  71.4 8.1 %collective-permute-start.1 = (bf16[256,128]{1,0:T(8,128)(2,1)S(1)}, bf16[256,128]{1,0:T(8,128)(2,1)S(1)}, u32[]{:S(2)}, u32[]{:S(2)}) collective-permute-start(bf16[256,128]{1,0:T(8,128)(2,1)S(1)} %get-tuple-element.753), channel_id=1, source_target_pairs={{240,0},{0,16},{16,32},{32,48},{48,64},{64,80},{80,96},{96,112},{1... | collective-permute-start | bytes 196616 | tf_op jit(solution)/shard_map/while/body/eval_jaxpr/ppermute | solution.py:15
  85.0 7.4 %collective-permute-start = (bf16[256,128]{1,0:T(8,128)(2,1)S(1)}, bf16[256,128]{1,0:T(8,128)(2,1)S(1)}, u32[]{:S(2)}, u32[]{:S(2)}) collective-permute-start(bf16[256,128]{1,0:T(8,128)(2,1)S(1)} %get-tuple-element.752), channel_id=1, source_target_pairs={{240,0},{0,16},{16,32},{32,48},{48,64},{64,80},{80,96},{96,112},{1... | collective-permute-start | bytes 196616 | tf_op jit(solution)/shard_map/while/body/eval_jaxpr/ppermute | solution.py:15
  85.2 8.1 %collective-permute-start.1 = (bf16[256,128]{1,0:T(8,128)(2,1)S(1)}, bf16[256,128]{1,0:T(8,128)(2,1)S(1)}, u32[]{:S(2)}, u32[]{:S(2)}) collective-permute-start(bf16[256,128]{1,0:T(8,128)(2,1)S(1)} %get-tuple-element.753), channel_id=1, source_target_pairs={{240,0},{0,16},{16,32},{32,48},{48,64},{64,80},{80,96},{96,112},{1... | collective-permute-start | bytes 196616 | tf_op jit(solution)/shard_map/while/body/eval_jaxpr/ppermute | solution.py:15
  98.8 7.4 %collective-permute-start = (bf16[256,128]{1,0:T(8,128)(2,1)S(1)}, bf16[256,128]{1,0:T(8,128)(2,1)S(1)}, u32[]{:S(2)}, u32[]{:S(2)}) collective-permute-start(bf16[256,128]{1,0:T(8,128)(2,1)S(1)} %get-tuple-element.752), channel_id=1, source_target_pairs={{240,0},{0,16},{16,32},{32,48},{48,64},{64,80},{80,96},{96,112},{1... | collective-permute-start | bytes 196616 | tf_op jit(solution)/shard_map/while/body/eval_jaxpr/ppermute | solution.py:15
  99.0 8.1 %collective-permute-start.1 = (bf16[256,128]{1,0:T(8,128)(2,1)S(1)}, bf16[256,128]{1,0:T(8,128)(2,1)S(1)}, u32[]{:S(2)}, u32[]{:S(2)}) collective-permute-start(bf16[256,128]{1,0:T(8,128)(2,1)S(1)} %get-tuple-element.753), channel_id=1, source_target_pairs={{240,0},{0,16},{16,32},{32,48},{48,64},{64,80},{80,96},{96,112},{1... | collective-permute-start | bytes 196616 | tf_op jit(solution)/shard_map/while/body/eval_jaxpr/ppermute | solution.py:15
  112.6 7.4 %collective-permute-start = (bf16[256,128]{1,0:T(8,128)(2,1)S(1)}, bf16[256,128]{1,0:T(8,128)(2,1)S(1)}, u32[]{:S(2)}, u32[]{:S(2)}) collective-permute-start(bf16[256,128]{1,0:T(8,128)(2,1)S(1)} %get-tuple-element.752), channel_id=1, source_target_pairs={{240,0},{0,16},{16,32},{32,48},{48,64},{64,80},{80,96},{96,112},{1... | collective-permute-start | bytes 196616 | tf_op jit(solution)/shard_map/while/body/eval_jaxpr/ppermute | solution.py:15
  112.8 8.1 %collective-permute-start.1 = (bf16[256,128]{1,0:T(8,128)(2,1)S(1)}, bf16[256,128]{1,0:T(8,128)(2,1)S(1)}, u32[]{:S(2)}, u32[]{:S(2)}) collective-permute-start(bf16[256,128]{1,0:T(8,128)(2,1)S(1)} %get-tuple-element.753), channel_id=1, source_target_pairs={{240,0},{0,16},{16,32},{32,48},{48,64},{64,80},{80,96},{96,112},{1... | collective-permute-start | bytes 196616 | tf_op jit(solution)/shard_map/while/body/eval_jaxpr/ppermute | solution.py:15
  126.4 7.4 %collective-permute-start = (bf16[256,128]{1,0:T(8,128)(2,1)S(1)}, bf16[256,128]{1,0:T(8,128)(2,1)S(1)}, u32[]{:S(2)}, u32[]{:S(2)}) collective-permute-start(bf16[256,128]{1,0:T(8,128)(2,1)S(1)} %get-tuple-element.752), channel_id=1, source_target_pairs={{240,0},{0,16},{16,32},{32,48},{48,64},{64,80},{80,96},{96,112},{1... | collective-permute-start | bytes 196616 | tf_op jit(solution)/shard_map/while/body/eval_jaxpr/ppermute | solution.py:15
  126.6 8.1 %collective-permute-start.1 = (bf16[256,128]{1,0:T(8,128)(2,1)S(1)}, bf16[256,128]{1,0:T(8,128)(2,1)S(1)}, u32[]{:S(2)}, u32[]{:S(2)}) collective-permute-start(bf16[256,128]{1,0:T(8,128)(2,1)S(1)} %get-tuple-element.753), channel_id=1, source_target_pairs={{240,0},{0,16},{16,32},{32,48},{48,64},{64,80},{80,96},{96,112},{1... | collective-permute-start | bytes 196616 | tf_op jit(solution)/shard_map/while/body/eval_jaxpr/ppermute | solution.py:15
  140.2 7.4 %collective-permute-start = (bf16[256,128]{1,0:T(8,128)(2,1)S(1)}, bf16[256,128]{1,0:T(8,128)(2,1)S(1)}, u32[]{:S(2)}, u32[]{:S(2)}) collective-permute-start(bf16[256,128]{1,0:T(8,128)(2,1)S(1)} %get-tuple-element.752), channel_id=1, source_target_pairs={{240,0},{0,16},{16,32},{32,48},{48,64},{64,80},{80,96},{96,112},{1... | collective-permute-start | bytes 196616 | tf_op jit(solution)/shard_map/while/body/eval_jaxpr/ppermute | solution.py:15
  140.4 8.1 %collective-permute-start.1 = (bf16[256,128]{1,0:T(8,128)(2,1)S(1)}, bf16[256,128]{1,0:T(8,128)(2,1)S(1)}, u32[]{:S(2)}, u32[]{:S(2)}) collective-permute-start(bf16[256,128]{1,0:T(8,128)(2,1)S(1)} %get-tuple-element.753), channel_id=1, source_target_pairs={{240,0},{0,16},{16,32},{32,48},{48,64},{64,80},{80,96},{96,112},{1... | collective-permute-start | bytes 196616 | tf_op jit(solution)/shard_map/while/body/eval_jaxpr/ppermute | solution.py:15
  154.0 7.4 %collective-permute-start = (bf16[256,128]{1,0:T(8,128)(2,1)S(1)}, bf16[256,128]{1,0:T(8,128)(2,1)S(1)}, u32[]{:S(2)}, u32[]{:S(2)}) collective-permute-start(bf16[256,128]{1,0:T(8,128)(2,1)S(1)} %get-tuple-element.752), channel_id=1, source_target_pairs={{240,0},{0,16},{16,32},{32,48},{48,64},{64,80},{80,96},{96,112},{1... | collective-permute-start | bytes 196616 | tf_op jit(solution)/shard_map/while/body/eval_jaxpr/ppermute | solution.py:15
  154.2 8.1 %collective-permute-start.1 = (bf16[256,128]{1,0:T(8,128)(2,1)S(1)}, bf16[256,128]{1,0:T(8,128)(2,1)S(1)}, u32[]{:S(2)}, u32[]{:S(2)}) collective-permute-start(bf16[256,128]{1,0:T(8,128)(2,1)S(1)} %get-tuple-element.753), channel_id=1, source_target_pairs={{240,0},{0,16},{16,32},{32,48},{48,64},{64,80},{80,96},{96,112},{1... | collective-permute-start | bytes 196616 | tf_op jit(solution)/shard_map/while/body/eval_jaxpr/ppermute | solution.py:15
  167.8 7.4 %collective-permute-start = (bf16[256,128]{1,0:T(8,128)(2,1)S(1)}, bf16[256,128]{1,0:T(8,128)(2,1)S(1)}, u32[]{:S(2)}, u32[]{:S(2)}) collective-permute-start(bf16[256,128]{1,0:T(8,128)(2,1)S(1)} %get-tuple-element.752), channel_id=1, source_target_pairs={{240,0},{0,16},{16,32},{32,48},{48,64},{64,80},{80,96},{96,112},{1... | collective-permute-start | bytes 196616 | tf_op jit(solution)/shard_map/while/body/eval_jaxpr/ppermute | solution.py:15
  168.0 8.1 %collective-permute-start.1 = (bf16[256,128]{1,0:T(8,128)(2,1)S(1)}, bf16[256,128]{1,0:T(8,128)(2,1)S(1)}, u32[]{:S(2)}, u32[]{:S(2)}) collective-permute-start(bf16[256,128]{1,0:T(8,128)(2,1)S(1)} %get-tuple-element.753), channel_id=1, source_target_pairs={{240,0},{0,16},{16,32},{32,48},{48,64},{64,80},{80,96},{96,112},{1... | collective-permute-start | bytes 196616 | tf_op jit(solution)/shard_map/while/body/eval_jaxpr/ppermute | solution.py:15
  181.6 7.4 %collective-permute-start = (bf16[256,128]{1,0:T(8,128)(2,1)S(1)}, bf16[256,128]{1,0:T(8,128)(2,1)S(1)}, u32[]{:S(2)}, u32[]{:S(2)}) collective-permute-start(bf16[256,128]{1,0:T(8,128)(2,1)S(1)} %get-tuple-element.752), channel_id=1, source_target_pairs={{240,0},{0,16},{16,32},{32,48},{48,64},{64,80},{80,96},{96,112},{1... | collective-permute-start | bytes 196616 | tf_op jit(solution)/shard_map/while/body/eval_jaxpr/ppermute | solution.py:15
  181.8 8.1 %collective-permute-start.1 = (bf16[256,128]{1,0:T(8,128)(2,1)S(1)}, bf16[256,128]{1,0:T(8,128)(2,1)S(1)}, u32[]{:S(2)}, u32[]{:S(2)}) collective-permute-start(bf16[256,128]{1,0:T(8,128)(2,1)S(1)} %get-tuple-element.753), channel_id=1, source_target_pairs={{240,0},{0,16},{16,32},{32,48},{48,64},{64,80},{80,96},{96,112},{1... | collective-permute-start | bytes 196616 | tf_op jit(solution)/shard_map/while/body/eval_jaxpr/ppermute | solution.py:15
  195.4 7.4 %collective-permute-start = (bf16[256,128]{1,0:T(8,128)(2,1)S(1)}, bf16[256,128]{1,0:T(8,128)(2,1)S(1)}, u32[]{:S(2)}, u32[]{:S(2)}) collective-permute-start(bf16[256,128]{1,0:T(8,128)(2,1)S(1)} %get-tuple-element.752), channel_id=1, source_target_pairs={{240,0},{0,16},{16,32},{32,48},{48,64},{64,80},{80,96},{96,112},{1... | collective-permute-start | bytes 196616 | tf_op jit(solution)/shard_map/while/body/eval_jaxpr/ppermute | solution.py:15
  195.6 8.1 %collective-permute-start.1 = (bf16[256,128]{1,0:T(8,128)(2,1)S(1)}, bf16[256,128]{1,0:T(8,128)(2,1)S(1)}, u32[]{:S(2)}, u32[]{:S(2)}) collective-permute-start(bf16[256,128]{1,0:T(8,128)(2,1)S(1)} %get-tuple-element.753), channel_id=1, source_target_pairs={{240,0},{0,16},{16,32},{32,48},{48,64},{64,80},{80,96},{96,112},{1... | collective-permute-start | bytes 196616 | tf_op jit(solution)/shard_map/while/body/eval_jaxpr/ppermute | solution.py:15
  209.2 7.4 %collective-permute-start = (bf16[256,128]{1,0:T(8,128)(2,1)S(1)}, bf16[256,128]{1,0:T(8,128)(2,1)S(1)}, u32[]{:S(2)}, u32[]{:S(2)}) collective-permute-start(bf16[256,128]{1,0:T(8,128)(2,1)S(1)} %get-tuple-element.752), channel_id=1, source_target_pairs={{240,0},{0,16},{16,32},{32,48},{48,64},{64,80},{80,96},{96,112},{1... | collective-permute-start | bytes 196616 | tf_op jit(solution)/shard_map/while/body/eval_jaxpr/ppermute | solution.py:15
  209.4 8.1 %collective-permute-start.1 = (bf16[256,128]{1,0:T(8,128)(2,1)S(1)}, bf16[256,128]{1,0:T(8,128)(2,1)S(1)}, u32[]{:S(2)}, u32[]{:S(2)}) collective-permute-start(bf16[256,128]{1,0:T(8,128)(2,1)S(1)} %get-tuple-element.753), channel_id=1, source_target_pairs={{240,0},{0,16},{16,32},{32,48},{48,64},{64,80},{80,96},{96,112},{1... | collective-permute-start | bytes 196616 | tf_op jit(solution)/shard_map/while/body/eval_jaxpr/ppermute | solution.py:15
  223.0 7.4 %collective-permute-start = (bf16[256,128]{1,0:T(8,128)(2,1)S(1)}, bf16[256,128]{1,0:T(8,128)(2,1)S(1)}, u32[]{:S(2)}, u32[]{:S(2)}) collective-permute-start(bf16[256,128]{1,0:T(8,128)(2,1)S(1)} %get-tuple-element.752), channel_id=1, source_target_pairs={{240,0},{0,16},{16,32},{32,48},{48,64},{64,80},{80,96},{96,112},{1... | collective-permute-start | bytes 196616 | tf_op jit(solution)/shard_map/while/body/eval_jaxpr/ppermute | solution.py:15
  223.2 8.1 %collective-permute-start.1 = (bf16[256,128]{1,0:T(8,128)(2,1)S(1)}, bf16[256,128]{1,0:T(8,128)(2,1)S(1)}, u32[]{:S(2)}, u32[]{:S(2)}) collective-permute-start(bf16[256,128]{1,0:T(8,128)(2,1)S(1)} %get-tuple-element.753), channel_id=1, source_target_pairs={{240,0},{0,16},{16,32},{32,48},{48,64},{64,80},{80,96},{96,112},{1... | collective-permute-start | bytes 196616 | tf_op jit(solution)/shard_map/while/body/eval_jaxpr/ppermute | solution.py:15
  236.8 7.4 %collective-permute-start = (bf16[256,128]{1,0:T(8,128)(2,1)S(1)}, bf16[256,128]{1,0:T(8,128)(2,1)S(1)}, u32[]{:S(2)}, u32[]{:S(2)}) collective-permute-start(bf16[256,128]{1,0:T(8,128)(2,1)S(1)} %get-tuple-element.752), channel_id=1, source_target_pairs={{240,0},{0,16},{16,32},{32,48},{48,64},{64,80},{80,96},{96,112},{1... | collective-permute-start | bytes 196616 | tf_op jit(solution)/shard_map/while/body/eval_jaxpr/ppermute | solution.py:15
  237.0 8.1 %collective-permute-start.1 = (bf16[256,128]{1,0:T(8,128)(2,1)S(1)}, bf16[256,128]{1,0:T(8,128)(2,1)S(1)}, u32[]{:S(2)}, u32[]{:S(2)}) collective-permute-start(bf16[256,128]{1,0:T(8,128)(2,1)S(1)} %get-tuple-element.753), channel_id=1, source_target_pairs={{240,0},{0,16},{16,32},{32,48},{48,64},{64,80},{80,96},{96,112},{1... | collective-permute-start | bytes 196616 | tf_op jit(solution)/shard_map/while/body/eval_jaxpr/ppermute | solution.py:15
  250.6 7.4 %collective-permute-start = (bf16[256,128]{1,0:T(8,128)(2,1)S(1)}, bf16[256,128]{1,0:T(8,128)(2,1)S(1)}, u32[]{:S(2)}, u32[]{:S(2)}) collective-permute-start(bf16[256,128]{1,0:T(8,128)(2,1)S(1)} %get-tuple-element.752), channel_id=1, source_target_pairs={{240,0},{0,16},{16,32},{32,48},{48,64},{64,80},{80,96},{96,112},{1... | collective-permute-start | bytes 196616 | tf_op jit(solution)/shard_map/while/body/eval_jaxpr/ppermute | solution.py:15
  250.8 8.1 %collective-permute-start.1 = (bf16[256,128]{1,0:T(8,128)(2,1)S(1)}, bf16[256,128]{1,0:T(8,128)(2,1)S(1)}, u32[]{:S(2)}, u32[]{:S(2)}) collective-permute-start(bf16[256,128]{1,0:T(8,128)(2,1)S(1)} %get-tuple-element.753), channel_id=1, source_target_pairs={{240,0},{0,16},{16,32},{32,48},{48,64},{64,80},{80,96},{96,112},{1... | collective-permute-start | bytes 196616 | tf_op jit(solution)/shard_map/while/body/eval_jaxpr/ppermute | solution.py:15
  265.2 11.0 %all-to-all-start.4 = ((f32[8,1,256]{2,1,0:T(1,128)}), f32[8,1,256]{2,1,0:T(1,128)S(1)}, u32[]{:S(2)}, u32[]{:S(2)}) async-start(f32[8,1,256]{2,1,0:T(1,128)} %reshape.596), calls=%async_computation.4 | async-start | bytes 16384 | tf_op jit(solution)/shard_map/all_to_all | solution.py:125
  276.2 20.3 %all-to-all-start.3 = ((bf16[8,32,1024]{2,1,0:T(8,128)(2,1)}), bf16[8,32,1024]{2,1,0:T(8,128)(2,1)S(1)}, u32[]{:S(2)}, u32[]{:S(2)}) async-start(bf16[8,32,1024]{2,1,0:T(8,128)(2,1)} %all_to_all.79), calls=%async_computation.3 | async-start | bytes 1048576 | tf_op jit(solution)/shard_map/all_to_all | solution.py:124
where the time goes:
time: 299 us; the launch traced here: 297 us
  matrix products  90.4 us (30%)
  starting transfers between devices  72 us (24%)
  waiting for transfers between devices  43.2 us (14%)
  loops' own time  40.2 us (13%)
  local copies, waits for them, and re-layouts  32.9 us (11%)
  other arithmetic  15.2 us (5%)
  between operations  3.4 us (1%)
    dot_general x32, matrix products, absorb(): jnp.einsum('kgts,skd->kgtd', rounded, value_head_count, preferred_element...  47.3 us
    ppermute x30, starting transfers between devices, passed_along(): return lax.ppermute(block, axis, route)  45.9 us
    another operation x1, loops' own time, local(): lax.fori_loop(1, cycle_size, cycle_turn, (state, head_keys, head_values))[0]  40.2 us
    dot_general x32, matrix products, absorb(): jnp.einsum('kgts,sk->kgt', rounded.astype(jnp.float32), value_check, prec...  33.2 us
    all_to_all x1, waiting for transfers between devices, local(): lax.all_to_all(output, 'head', split_axis=0, concat_axis=1, tiled=True)  14.8 us
    all_to_all x1, waiting for transfers between devices, local(): lax.all_to_all(queries, 'head', split_axis=1, concat_axis=0, tiled=True)  14.1 us
    dynamic_slice x16, local copies, waits for them, and re-layouts, absorb(): lax.dynamic_index_in_dim(value_block_scale, span_number, 0, keepdims=False)  10.7 us
    dynamic_slice x16, local copies, waits for them, and re-layouts, absorb(): lax.dynamic_index_in_dim(span_order, span_number, 0, keepdims=False)  10.6 us
  transfers between devices with their start and end apart: 35, of which 4 were waited for; matrix products, arithmetic and copies ran while one was open for 16% of the time, Pallas kernels for 0%

commit v1 on v0

v1 whole, which is shorter than its diff:
```python
import math

import jax
import jax.numpy as jnp
from jax import lax
from jax.experimental import pallas as pl
from jax.experimental.pallas import tpu as pltpu
from jax.sharding import PartitionSpec as P

HEAD_WIDTH = 128
SPAN = 128
HEADS = 8
CTX = 16
SHARE = 256
KEYS = CTX * SHARE
PIECE = 32
ROWS = HEADS * PIECE
AUG = 144
FAR = 1e30
INVERSE_ROOT = 1.0 / math.sqrt(HEAD_WIDTH)
SCORE_FACTOR = INVERSE_ROOT * 1.4426950408889634
KEY_CHUNK = 512
MESH = pl.DeviceIdType.MESH


def kernel(
    q_hbm, k_hbm, v_hbm, ks_ref, vs_ref, order_ref, keep_ref,
    out_hbm, chk_out,
    qbuf, kbuf, vbuf, vt, scores, ostage, cstage, crecv,
    loc_sem, kv_send, kv_recv, q_send, q_recv,
    x_send, x_recv, y_send, y_recv, f_send, f_recv, c_send, c_recv,
    o_send, o_recv, h_send, h_recv,
):
    ctx = lax.axis_index("ctx")
    me = lax.axis_index("head")
    core = lax.rem(ctx, 2)
    xh = lax.rem(ctx // 2, 2)
    y = ctx // 4

    def place(py, px, pc):
        return (py * 2 + px) * 2 + pc

    y_up, y_down, y_far = lax.rem(y + 1, 4), lax.rem(y + 3, 4), lax.rem(y + 2, 4)
    up = {"ctx": place(y_up, xh, core)}
    down = {"ctx": place(y_down, xh, core)}
    across = {"ctx": place(y, 1 - xh, core)}
    sibling = {"ctx": place(y, xh, 1 - core)}

    def peer(d):
        return {"head": lax.rem(me + d, HEADS)}

    def remote(src, dst, send, recv, device):
        return pltpu.make_async_remote_copy(
            src_ref=src, dst_ref=dst, send_sem=send, recv_sem=recv,
            device_id=device, device_id_type=MESH,
        )

    barrier = pltpu.get_barrier_semaphore()
    for d in range(1, HEADS):
        pl.semaphore_signal(barrier, inc=1, device_id=peer(d), device_id_type=MESH)
    for device in (up, down, across, sibling):
        pl.semaphore_signal(barrier, inc=1, device_id=device, device_id_type=MESH)
    pl.semaphore_wait(barrier, HEADS - 1 + 4)

    def rows_of(share, piece=0, size=SHARE):
        return pl.ds(pl.multiple_of(share * SHARE + piece * PIECE, PIECE), size)

    def columns_of(group, width):
        return pl.ds(pl.multiple_of(group * width, width), width)

    order = [1, 7, 2, 6, 3, 5, 4]
    landing = rows_of(ctx, me, PIECE)
    own_k = pltpu.make_async_copy(k_hbm.at[:, columns_of(me, 128)], kbuf.at[landing], loc_sem.at[0])
    own_v = pltpu.make_async_copy(v_hbm.at[:, columns_of(me, 128)], vbuf.at[landing], loc_sem.at[1])
    own_q = pltpu.make_async_copy(q_hbm.at[:, columns_of(me, 1024)], qbuf.at[0], loc_sem.at[2])
    kv_copies, q_copies = {}, {}
    for d in range(1, HEADS):
        to = lax.rem(me + d, HEADS)
        kv_copies[d] = (
            remote(k_hbm.at[:, columns_of(to, 128)], kbuf.at[landing],
                   kv_send.at[0, d], kv_recv.at[0, d], peer(d)),
            remote(v_hbm.at[:, columns_of(to, 128)], vbuf.at[landing],
                   kv_send.at[1, d], kv_recv.at[1, d], peer(d)),
        )
        q_copies[d] = remote(q_hbm.at[:, columns_of(to, 1024)], qbuf.at[d],
                             q_send.at[d], q_recv.at[d], peer(d))
    for d in reversed(order):
        kv_copies[d][0].start()
        kv_copies[d][1].start()
    own_k.start()
    own_v.start()
    own_q.start()
    for d in order:
        q_copies[d].start()

    own_k.wait()
    own_v.wait()
    for d in order:
        kv_copies[d][0].wait_recv()
        kv_copies[d][1].wait_recv()

    def pair(share, send, recv, device):
        rows = rows_of(share)
        return [
            remote(kbuf.at[rows], kbuf.at[rows], send.at[0], recv.at[0], device),
            remote(vbuf.at[rows], vbuf.at[rows], send.at[1], recv.at[1], device),
        ]

    sent = []

    def go(copies):
        for copy in copies:
            copy.start()
        sent.extend(copies)

    own = place(y, xh, core)
    x_pair = pair(own, x_send, x_recv, across)
    go(x_pair)
    sibling_copies = []

    def tell(share, slot):
        copies = pair(share, c_send.at[slot], c_recv.at[slot], sibling)
        go(copies)
        sibling_copies.append(copies)

    for line in range(2):
        px = xh if line == 0 else 1 - xh
        if line == 1:
            x_pair[0].wait_recv()
            x_pair[1].wait_recv()
        here = place(y, px, core)
        to_up = pair(here, y_send.at[line, 0], y_recv.at[line, 0], up)
        to_down = pair(here, y_send.at[line, 1], y_recv.at[line, 1], down)
        go(to_up)
        go(to_down[::-1])
        tell(here, 4 * line)
        below, above = place(y_down, px, core), place(y_up, px, core)
        rows_below, rows_above = rows_of(below), rows_of(above)
        forward_k = remote(kbuf.at[rows_below], kbuf.at[rows_below],
                           f_send.at[line, 0], f_recv.at[line, 0], up)
        forward_v = remote(vbuf.at[rows_above], vbuf.at[rows_above],
                           f_send.at[line, 1], f_recv.at[line, 1], down)
        to_up[0].wait_recv()
        go([forward_k])
        to_down[1].wait_recv()
        go([forward_v])
        to_up[1].wait_recv()
        tell(below, 4 * line + 1)
        to_down[0].wait_recv()
        tell(above, 4 * line + 2)
        forward_k.wait_recv()
        forward_v.wait_recv()
        tell(place(y_far, px, core), 4 * line + 3)
    for copies in sibling_copies:
        copies[0].wait_recv()
        copies[1].wait_recv()

    def turn_values(block, carry):
        rows = pl.ds(pl.multiple_of(block * SPAN, SPAN), SPAN)
        turned = vbuf[rows, :].astype(jnp.float32).T
        factor = vs_ref[block]
        vt[0:HEAD_WIDTH, rows] = (turned * factor).astype(jnp.bfloat16)
        check = jnp.sum(turned, axis=0, keepdims=True) * factor * INVERSE_ROOT
        high = check.astype(jnp.bfloat16).astype(jnp.float32)
        row = lax.broadcasted_iota(jnp.int32, (16, SPAN), 0)
        extra = jnp.where(
            row == 0, 1.0,
            jnp.where(row == 1, jnp.broadcast_to(high, (16, SPAN)),
                      jnp.where(row == 2, jnp.broadcast_to(check - high, (16, SPAN)), 0.0)),
        )
        vt[HEAD_WIDTH:AUG, rows] = extra.astype(jnp.bfloat16)
        return carry

    lax.fori_loop(0, KEYS // SPAN, turn_values, 0)

    own_q.wait()

    def out_copy(slot):
        to = {"head": lax.rem(me - slot + HEADS, HEADS)}
        return (
            remote(ostage.at[slot], out_hbm.at[:, columns_of(me, 1024)],
                   o_send.at[slot], o_recv.at[slot], to),
            remote(cstage.at[slot], crecv.at[me], h_send.at[slot], h_recv.at[slot], to),
        )

    own_out = (
        pltpu.make_async_copy(ostage.at[0], out_hbm.at[:, columns_of(me, 1024)], loc_sem.at[3]),
        pltpu.make_async_copy(cstage.at[0], crecv.at[me], loc_sem.at[4]),
    )

    def chunk(step, carry):
        half = (step + 1) // 2
        slot = lax.rem(half * (1 - 2 * lax.rem(step + 1, 2)) + HEADS, HEADS)
        source = lax.rem(me - slot + HEADS, HEADS)

        @pl.when(step > 0)
        def _():
            remote(qbuf.at[slot], qbuf.at[slot], q_send.at[slot], q_recv.at[slot],
                   {"head": lax.rem(me + slot, HEADS)}).wait_recv()

        own_block = 2 * ctx + source // 4
        own_order = order_ref[own_block]
        query_rows = jnp.concatenate(
            [qbuf[slot, :, 128 * j : 128 * (j + 1)] for j in range(HEADS)], axis=0
        )

        def bias(block):
            seen = (keep_ref[own_block, block] > 0) & (own_order > order_ref[block])
            return jnp.where(seen, jnp.float32(0.0), jnp.float32(FAR))

        highest = jnp.full((8, ROWS), -FAR, jnp.float32)
        for start in range(0, KEYS, KEY_CHUNK):
            part = lax.dot_general(
                kbuf[start : start + KEY_CHUNK, :], query_rows, (((1,), (1,)), ((), ())),
                preferred_element_type=jnp.float32,
            )
            scores[start : start + KEY_CHUNK, :] = part
            for i in range(KEY_CHUNK // SPAN):
                block = start // SPAN + i
                top = jnp.max(part[i * SPAN : (i + 1) * SPAN].reshape(16, 8, ROWS), axis=0)
                highest = jnp.maximum(highest, top * (ks_ref[block] * SCORE_FACTOR) - bias(block))
        own_rows = pl.ds(pl.multiple_of(own_block * SPAN, SPAN), SPAN)
        key_place = lax.broadcasted_iota(jnp.int32, (SPAN, ROWS), 0)
        query_place = PIECE * lax.rem(source, 4) + lax.rem(
            lax.broadcasted_iota(jnp.int32, (SPAN, ROWS), 1), PIECE
        )
        own_scores = jnp.where(key_place <= query_place, scores[own_rows, :], -FAR)
        scores[own_rows, :] = own_scores
        top = jnp.max(own_scores.reshape(16, 8, ROWS), axis=0)
        highest = jnp.maximum(highest, top * (ks_ref[own_block] * SCORE_FACTOR))
        peak = jnp.max(highest, axis=0, keepdims=True)
        mixed = jnp.zeros((AUG, ROWS), jnp.float32)
        for start in range(0, KEYS, KEY_CHUNK):
            weights = []
            for i in range(KEY_CHUNK // SPAN):
                block = start // SPAN + i
                hidden = jnp.where(own_block == block, jnp.float32(0.0), bias(block))
                part = scores[block * SPAN : (block + 1) * SPAN, :]
                weights.append(
                    jnp.exp2(part * (ks_ref[block] * SCORE_FACTOR) - (peak + hidden)).astype(jnp.bfloat16)
                )
            mixed = mixed + lax.dot_general(
                vt[:, start : start + KEY_CHUNK], jnp.concatenate(weights, axis=0),
                (((1,), (0,)), ((), ())), preferred_element_type=jnp.float32,
            )
        share = 1.0 / mixed[HEAD_WIDTH : HEAD_WIDTH + 1]
        result = (mixed[0:HEAD_WIDTH] * share).T.astype(jnp.bfloat16)
        check = (mixed[HEAD_WIDTH + 1 : HEAD_WIDTH + 2] + mixed[HEAD_WIDTH + 2 : HEAD_WIDTH + 3]) * share
        for j in range(HEADS):
            ostage[slot, :, 128 * j : 128 * (j + 1)] = result[PIECE * j : PIECE * (j + 1)]
            cstage[slot, j : j + 1, 0:PIECE] = check[:, PIECE * j : PIECE * (j + 1)]

        @pl.when(step == 0)
        def _():
            own_out[0].start()
            own_out[1].start()

        @pl.when(step > 0)
        def _():
            copies = out_copy(slot)
            copies[0].start()
            copies[1].start()

        return carry

    lax.fori_loop(0, HEADS, chunk, 0)

    own_out[0].wait()
    own_out[1].wait()
    for d in order:
        copies = out_copy(d)
        copies[1].wait_recv()
    table = crecv[...].reshape(HEADS * HEADS, 128).T
    chk_out[...] = table[0:PIECE, :]
    for d in order:
        copies = out_copy(d)
        copies[0].wait_recv()
        copies[0].wait_send()
        copies[1].wait_send()
        kv_copies[d][0].wait_send()
        kv_copies[d][1].wait_send()
        q_copies[d].wait_send()
    for copy in sent:
        copy.wait_send()


def local(queries, unscaled_key_rows, unscaled_value_rows, key_block_scale, value_block_scale,
          span_order, block_keep):
    vmem = pl.BlockSpec(memory_space=pltpu.VMEM)
    smem = pl.BlockSpec(memory_space=pltpu.SMEM)
    anywhere = pl.BlockSpec(memory_space=pl.ANY)
    dma = pltpu.SemaphoreType.DMA
    return pl.pallas_call(
        kernel,
        out_shape=(
            jax.ShapeDtypeStruct((PIECE, 8192), jnp.bfloat16),
            jax.ShapeDtypeStruct((PIECE, 64), jnp.float32),
        ),
        in_specs=[anywhere, anywhere, anywhere, smem, smem, smem, smem],
        out_specs=(anywhere, vmem),
        scratch_shapes=[
            pltpu.VMEM((HEADS, PIECE, 1024), jnp.bfloat16),
            pltpu.VMEM((KEYS, HEAD_WIDTH), jnp.bfloat16),
            pltpu.VMEM((KEYS, HEAD_WIDTH), jnp.bfloat16),
            pltpu.VMEM((AUG, KEYS), jnp.bfloat16),
            pltpu.VMEM((KEYS, ROWS), jnp.float32),
            pltpu.VMEM((HEADS, PIECE, 1024), jnp.bfloat16),
            pltpu.VMEM((HEADS, HEADS, 128), jnp.float32),
            pltpu.VMEM((HEADS, HEADS, 128), jnp.float32),
            dma((5,)),
            dma((2, HEADS)), dma((2, HEADS)),
            dma((HEADS,)), dma((HEADS,)),
            dma((2,)), dma((2,)),
            dma((2, 2, 2)), dma((2, 2, 2)),
            dma((2, 2)), dma((2, 2)),
            dma((8, 2)), dma((8, 2)),
            dma((HEADS,)), dma((HEADS,)),
            dma((HEADS,)), dma((HEADS,)),
        ],
        compiler_params=pltpu.CompilerParams(
            collective_id=0, has_side_effects=True, vmem_limit_bytes=40 << 20
        ),
    )(
        queries, unscaled_key_rows, unscaled_value_rows,
        key_block_scale.reshape(32), value_block_scale.reshape(32), span_order, block_keep,
    )


def solution(mesh):
    rows = P(("dp", "ctx", "head"), None)
    return jax.shard_map(
        local,
        mesh=mesh,
        in_specs=(rows, rows, rows, P("dp", "head"), P("dp", "head"), P(), P()),
        out_specs=(rows, rows),
        check_vma=False,
    )
```

time: 299 us -> 67.8 us (0.23)
  the two profiles are of different devices: /device:TPU:30 before, /device:TPU:1 now
where the time goes in v1:
time: 67.8 us; the launch traced here: 66.6 us
  Pallas kernels  60.4 us (89%)
  local copies, waits for them, and re-layouts  5.5 us (8%)
    pallas_call x1, Pallas kernels, local(): pl.pallas_call(kernel, out_shape=(jax.ShapeDtypeStruct((PIECE, 8192), jnp...  60.4 us
    unnamed x16, local copies, waits for them, and re-layouts  5.5 us

profile of v1, /device:TPU:1, one launch (start us, length us, event | category | flops | bytes accessed | tf_op | source)
XLA Modules:
  0.0 66.6 jit_solution(7886401256036803343)
XLA Ops:
  0.6 0.0 copy-start.4
  0.6 0.0 copy-start.5
  0.7 0.0 copy-start.6
  0.7 0.6 copy-done.4
  1.3 0.0 copy-done.5
  1.3 0.0 copy-done.6
  1.3 0.0 copy-start
  1.3 1.0 %copy-done = bf16[32,8192]{1,0:T(8,128)(2,1)S(1)} copy-done((bf16[32,8192]{1,0:T(8,128)(2,1)S(1)}, bf16[32,8192]{1,0:T(8,128)(2,1)}, u32[]{:S(2)}) %copy-start) | copy-done | bytes 524312
  2.4 0.0 copy-start.1
  2.4 0.8 %copy-done.1 = bf16[32,1024]{1,0:T(8,128)(2,1)S(1)} copy-done((bf16[32,1024]{1,0:T(8,128)(2,1)S(1)}, bf16[32,1024]{1,0:T(8,128)(2,1)}, u32[]{:S(2)}) %copy-start.1) | copy-done | bytes 65560
  3.2 0.0 copy-start.2
  3.2 0.8 %copy-done.2 = bf16[32,1024]{1,0:T(8,128)(2,1)S(1)} copy-done((bf16[32,1024]{1,0:T(8,128)(2,1)S(1)}, bf16[32,1024]{1,0:T(8,128)(2,1)}, u32[]{:S(2)}) %copy-start.2) | copy-done | bytes 65560
  4.0 0.0 copy-start.3
  4.0 0.7 %copy-done.3 = s32[32,32]{1,0:T(8,128)S(1)} copy-done((s32[32,32]{1,0:T(8,128)S(1)}, s32[32,32]{1,0:T(8,128)}, u32[]{:S(2)}) %copy-start.3) | copy-done | bytes 4120
  4.8 60.4 %shard_map.86 = (bf16[32,8192]{1,0:T(8,128)(2,1)S(1)}, f32[32,64]{1,0:T(8,128)S(1)}) custom-call(bf16[32,8192]{1,0:T(8,128)(2,1)S(1)} %copy-done, bf16[32,1024]{1,0:T(8,128)(2,1)S(1)} %copy-done.1, bf16[32,1024]{1,0:T(8,128)(2,1)S(1)} %copy-done.2, f32[32]{0:T(128)S(1)} %bitcast.2, f32[32]{0:T(128)S(1)} %bitcast.3, s32[32]{0:T(128)S(1)} %copy-done.6, ...), custom_call_target="tpu_custom_call" | custom-call | tf_op jit(solution)/shard_map/pallas_call | solution.py:293
  65.2 0.8 %copy.11 = bf16[32,8192]{1,0:T(8,128)(2,1)} copy(bf16[32,8192]{1,0:T(8,128)(2,1)S(1)} %get-tuple-element.4) | data formatting | bytes 1048576
  66.0 0.6 copy.12
Async XLA Ops:
  0.6 0.7 copy-start.4
  0.6 0.7 copy-start.5
  0.7 0.7 %copy-start.6 = (s32[32]{0:T(128)S(1)}, s32[32]{0:T(128)}, u32[]{:S(2)}) copy-start(s32[32]{0:T(128)} %order_ref.1) | copy-start | bytes 388
  1.3 1.0 %copy-start = (bf16[32,8192]{1,0:T(8,128)(2,1)S(1)}, bf16[32,8192]{1,0:T(8,128)(2,1)}, u32[]{:S(2)}) copy-start(bf16[32,8192]{1,0:T(8,128)(2,1)} %q_hbm.1) | copy-start | bytes 1572868
  2.4 0.8 %copy-start.1 = (bf16[32,1024]{1,0:T(8,128)(2,1)S(1)}, bf16[32,1024]{1,0:T(8,128)(2,1)}, u32[]{:S(2)}) copy-start(bf16[32,1024]{1,0:T(8,128)(2,1)} %k_hbm.1) | copy-start | bytes 196612
  3.2 0.8 %copy-start.2 = (bf16[32,1024]{1,0:T(8,128)(2,1)S(1)}, bf16[32,1024]{1,0:T(8,128)(2,1)}, u32[]{:S(2)}) copy-start(bf16[32,1024]{1,0:T(8,128)(2,1)} %v_hbm.1) | copy-start | bytes 196612
  4.0 0.7 %copy-start.3 = (s32[32,32]{1,0:T(8,128)S(1)}, s32[32,32]{1,0:T(8,128)}, u32[]{:S(2)}) copy-start(s32[32,32]{1,0:T(8,128)} %keep_ref.1) | copy-start | bytes 12292

commit v2 on v1

v2 whole, which is shorter than its diff:
```python
import math

import jax
import jax.numpy as jnp
from jax import lax
from jax.experimental import pallas as pl
from jax.experimental.pallas import tpu as pltpu
from jax.sharding import PartitionSpec as P

HEAD_WIDTH = 128
SPAN = 128
HEADS = 8
CTX = 16
SHARE = 256
KEYS = CTX * SHARE
PIECE = 32
ROWS = HEADS * PIECE
AUG = 144
FAR = 1e30
INVERSE_ROOT = 1.0 / math.sqrt(HEAD_WIDTH)
SCORE_FACTOR = INVERSE_ROOT * 1.4426950408889634
HALF = KEYS // 2
KEY_CHUNK = 512
MESH = pl.DeviceIdType.MESH


def kernel(
    q_hbm, k_hbm, v_hbm, ks_hbm, vs_hbm, order_hbm, keep_hbm,
    out_ref, chk_out,
    ks_ref, vs_ref, order_ref, keep_ref, bias_ref, factor_ref, vfactor_ref,
    qbuf, kbuf, vbuf, vt, scores, total, peaks, ostage, cstage, crecv,
    tab_sem, loc_sem, kv_send, kv_recv, q_send, q_recv,
    x_send, x_recv, y_send, y_recv, f_send, f_recv, c_send, c_recv,
    o_send, o_recv, h_send, h_recv,
):
    ctx = lax.axis_index("ctx")
    me = lax.axis_index("head")
    core = lax.rem(ctx, 2)
    xh = lax.rem(ctx // 2, 2)
    y = ctx // 4

    def place(py, px, pc):
        return (py * 2 + px) * 2 + pc

    ys = (y, lax.rem(y + 3, 4), lax.rem(y + 1, 4), lax.rem(y + 2, 4))
    up = {"ctx": place(ys[2], xh, core)}
    down = {"ctx": place(ys[1], xh, core)}
    across = {"ctx": place(y, 1 - xh, core)}
    sibling = {"ctx": place(y, xh, 1 - core)}

    def peer(d):
        return {"head": lax.rem(me + d, HEADS)}

    def remote(src, dst, send, recv, device):
        return pltpu.make_async_remote_copy(
            src_ref=src, dst_ref=dst, send_sem=send, recv_sem=recv,
            device_id=device, device_id_type=MESH,
        )

    barrier = pltpu.get_barrier_semaphore()
    for d in range(1, HEADS):
        pl.semaphore_signal(barrier, inc=1, device_id=peer(d), device_id_type=MESH)
    for device in (up, down, across, sibling):
        pl.semaphore_signal(barrier, inc=1, device_id=device, device_id_type=MESH)

    def columns_of(group, width):
        return pl.ds(pl.multiple_of(group * width, width), width)

    tables = [
        pltpu.make_async_copy(source, target, tab_sem.at[i])
        for i, (source, target) in enumerate(
            ((ks_hbm, ks_ref), (vs_hbm, vs_ref), (order_hbm, order_ref), (keep_hbm, keep_ref))
        )
    ]
    landing = pl.ds(pl.multiple_of(me * PIECE, PIECE), PIECE)
    own_k = pltpu.make_async_copy(k_hbm.at[:, columns_of(me, 128)], kbuf.at[landing], loc_sem.at[0])
    own_v = pltpu.make_async_copy(v_hbm.at[:, columns_of(me, 128)], vbuf.at[landing], loc_sem.at[1])
    own_q = pltpu.make_async_copy(q_hbm.at[:, columns_of(me, 1024)], qbuf.at[0], loc_sem.at[2])
    for copy in tables + [own_k, own_v, own_q]:
        copy.start()
    pl.semaphore_wait(barrier, HEADS - 1 + 4)

    order = [1, 7, 2, 6, 3, 5, 4]
    k_copies, v_copies, q_copies = {}, {}, {}
    for d in range(1, HEADS):
        to = lax.rem(me + d, HEADS)
        k_copies[d] = remote(k_hbm.at[:, columns_of(to, 128)], kbuf.at[landing],
                             kv_send.at[0, d], kv_recv.at[0, d], peer(d))
        v_copies[d] = remote(v_hbm.at[:, columns_of(to, 128)], vbuf.at[landing],
                             kv_send.at[1, d], kv_recv.at[1, d], peer(d))
        q_copies[d] = remote(q_hbm.at[:, columns_of(to, 1024)], qbuf.at[d],
                             q_send.at[d], q_recv.at[d], peer(d))
    for d in reversed(order):
        k_copies[d].start()
    for d in reversed(order):
        v_copies[d].start()
    for d in order:
        q_copies[d].start()

    bufs = (kbuf, vbuf)

    def rows_of(slot):
        return pl.ds(slot * SHARE, SHARE)

    def ship(kind, slot, to_slot, send, recv, device):
        return remote(bufs[kind].at[rows_of(slot)], bufs[kind].at[rows_of(to_slot)], send, recv, device)

    def x_copy(kind):
        return ship(kind, 0, 8, x_send.at[kind], x_recv.at[kind], across)

    def y_copy(line, way, kind):
        return ship(kind, 8 * line, 8 * line + 2 + 2 * way, y_send.at[line, way, kind],
                    y_recv.at[line, way, kind], (up, down)[way])

    def f_copy(line, kind):
        return ship(kind, 8 * line + 2 + 2 * kind, 8 * line + 6, f_send.at[line, kind],
                    f_recv.at[line, kind], (up, down)[kind])

    def c_copy(slot, kind):
        return ship(kind, slot, slot + 1, c_send.at[slot // 2, kind], c_recv.at[slot // 2, kind], sibling)

    own_k.wait()
    for d in order:
        k_copies[d].wait_recv()
    x_copy(0).start()
    y_copy(0, 0, 0).start()
    y_copy(0, 1, 0).start()
    c_copy(0, 0).start()
    own_v.wait()
    for d in order:
        v_copies[d].wait_recv()
    x_copy(1).start()
    y_copy(0, 1, 1).start()
    y_copy(0, 0, 1).start()
    c_copy(0, 1).start()

    for copy in tables:
        copy.wait()
    for slot in range(CTX):
        at = place(ys[slot % 8 // 2], xh if slot < 8 else 1 - xh, core if slot % 2 == 0 else 1 - core)
        for i in range(2):
            block = 2 * at + i
            factor_ref[2 * slot + i] = ks_ref[block] * SCORE_FACTOR
            vfactor_ref[2 * slot + i] = vs_ref[block]
            for q in range(2):
                seen = (keep_ref[2 * ctx + q, block] > 0) & (order_ref[2 * ctx + q] > order_ref[block])
                bias_ref[q, 2 * slot + i] = jnp.where(seen, jnp.float32(0.0), jnp.float32(FAR))

    def ring_on(line):
        y_copy(line, 0, 0).wait_recv()
        f_copy(line, 0).start()
        y_copy(line, 1, 1).wait_recv()
        f_copy(line, 1).start()
        c_copy(8 * line + 2, 0).start()
        c_copy(8 * line + 4, 1).start()
        y_copy(line, 1, 0).wait_recv()
        c_copy(8 * line + 4, 0).start()
        y_copy(line, 0, 1).wait_recv()
        c_copy(8 * line + 2, 1).start()

    def ring_end(line):
        for kind in range(2):
            f_copy(line, kind).wait_recv()
            c_copy(8 * line + 6, kind).start()

    def from_sibling(line):
        for slot in range(8 * line, 8 * line + 8, 2):
            for kind in range(2):
                c_copy(slot, kind).wait_recv()

    turn = (
        lax.broadcasted_iota(jnp.int32, (AUG, HEAD_WIDTH), 0)
        == lax.broadcasted_iota(jnp.int32, (AUG, HEAD_WIDTH), 1)
    ) | (lax.broadcasted_iota(jnp.int32, (AUG, HEAD_WIDTH), 0) >= HEAD_WIDTH)
    turn = jnp.where(turn, 1.0, 0.0).astype(jnp.bfloat16)

    def turn_values(slot, carry):
        rows = pl.ds(pl.multiple_of(slot * SHARE, SHARE), SHARE)
        turned = lax.dot_general(turn, vbuf[rows, :], (((1,), (1,)), ((), ())),
                                 preferred_element_type=jnp.float32)
        lane = lax.broadcasted_iota(jnp.int32, (1, SHARE), 1)
        factor = jnp.where(lane < SPAN, vfactor_ref[2 * slot], vfactor_ref[2 * slot + 1])
        vt[0:HEAD_WIDTH, rows] = (turned[0:HEAD_WIDTH] * factor).astype(jnp.bfloat16)
        check = turned[HEAD_WIDTH:AUG] * (factor * INVERSE_ROOT)
        high = check.astype(jnp.bfloat16).astype(jnp.float32)
        row = lax.broadcasted_iota(jnp.int32, (16, SHARE), 0)
        extra = jnp.where(row == 0, 1.0, jnp.where(row == 1, high, jnp.where(row == 2, check - high, 0.0)))
        vt[HEAD_WIDTH:AUG, rows] = extra.astype(jnp.bfloat16)
        return carry

    ring_on(0)
    for kind in range(2):
        x_copy(kind).wait_recv()
        y_copy(1, kind, kind).start()
        y_copy(1, 1 - kind, kind).start()
        c_copy(8, kind).start()
    ring_end(0)
    from_sibling(0)
    lax.fori_loop(0, 8, turn_values, 0)
    own_q.wait()

    def slot_of(step):
        half = (step + 1) // 2
        return lax.rem(half * (1 - 2 * lax.rem(step + 1, 2)) + HEADS, HEADS)

    def load_queries(slot):
        return jnp.concatenate(
            [qbuf[slot, :, 128 * j : 128 * (j + 1)] for j in range(HEADS)], axis=0
        )

    def block_top(part):
        return jnp.max(part.reshape(SPAN // 8, 8, ROWS), axis=0)

    def score_pass(line, slot, own_half, query_place):
        query_rows = load_queries(slot)
        highest = jnp.full((8, ROWS), -FAR, jnp.float32)
        for start in range(0, HALF, KEY_CHUNK):
            base = line * HALF + start
            part = lax.dot_general(
                kbuf[base : base + KEY_CHUNK, :], query_rows, (((1,), (1,)), ((), ())),
                preferred_element_type=jnp.float32,
            )
            for i in range(KEY_CHUNK // SPAN):
                block = base // SPAN + i
                piece = part[i * SPAN : (i + 1) * SPAN]
                bias = bias_ref[own_half, block]
                if block < 2:
                    free = jnp.where(bias > 0.0, -1, SPAN)
                    limit = jnp.where(own_half == block, query_place, free)
                    key_place = lax.broadcasted_iota(jnp.int32, (SPAN, ROWS), 0)
                    piece = jnp.where(key_place <= limit, piece, -FAR)
                    bias = 0.0
                scores[start + i * SPAN : start + (i + 1) * SPAN, :] = piece
                highest = jnp.maximum(highest, block_top(piece) * factor_ref[block] - bias)
        return jnp.max(highest, axis=0, keepdims=True)

    def value_pass(line, own_half, peak):
        mixed = jnp.zeros((AUG, ROWS), jnp.float32)
        for start in range(0, HALF, KEY_CHUNK):
            base = line * HALF + start
            weights = []
            for i in range(KEY_CHUNK // SPAN):
                block = base // SPAN + i
                bias = 0.0 if block < 2 else bias_ref[own_half, block]
                part = scores[start + i * SPAN : start + (i + 1) * SPAN, :]
                weights.append(jnp.exp2(part * factor_ref[block] - (peak + bias)).astype(jnp.bfloat16))
            mixed = mixed + lax.dot_general(
                vt[:, base : base + KEY_CHUNK], jnp.concatenate(weights, axis=0),
                (((1,), (0,)), ((), ())), preferred_element_type=jnp.float32,
            )
        return mixed

    def place_of_queries(source):
        return PIECE * lax.rem(source, 4) + lax.rem(lax.broadcasted_iota(jnp.int32, (1, ROWS), 1), PIECE)

    def first_half(step, carry):
        slot = slot_of(step)
        source = lax.rem(me - slot + HEADS, HEADS)

        @pl.when(step == 1)
        def _():
            ring_on(1)

        @pl.when(step == 4)
        def _():
            ring_end(1)

        @pl.when(step > 0)
        def _():
            remote(qbuf.at[slot], qbuf.at[slot], q_send.at[slot], q_recv.at[slot], peer(slot)).wait_recv()

        peak = score_pass(0, slot, source // 4, place_of_queries(source))
        peaks[slot] = jnp.broadcast_to(peak, (8, ROWS))
        total[slot] = value_pass(0, source // 4, peak)
        return carry

    lax.fori_loop(0, HEADS, first_half, 0)
    from_sibling(1)
    lax.fori_loop(8, CTX, turn_values, 0)

    def out_copy(slot):
        to = {"head": lax.rem(me - slot + HEADS, HEADS)}
        return (
            remote(ostage.at[slot], out_ref.at[:, columns_of(me, 1024)],
                   o_send.at[slot], o_recv.at[slot], to),
            remote(cstage.at[slot], crecv.at[me], h_send.at[slot], h_recv.at[slot], to),
        )

    def second_half(back, carry):
        step = HEADS - 1 - back
        slot = slot_of(step)
        source = lax.rem(me - slot + HEADS, HEADS)
        first_peak = peaks[slot][0:1]
        peak = jnp.maximum(first_peak, score_pass(1, slot, source // 4, None))
        mixed = total[slot] * jnp.exp2(first_peak - peak) + value_pass(1, source // 4, peak)
        share = 1.0 / mixed[HEAD_WIDTH : HEAD_WIDTH + 1]
        result = (mixed[0:HEAD_WIDTH] * share).T.astype(jnp.bfloat16)
        check = (mixed[HEAD_WIDTH + 1 : HEAD_WIDTH + 2] + mixed[HEAD_WIDTH + 2 : HEAD_WIDTH + 3]) * share

        @pl.when(step > 0)
        def _():
            for j in range(HEADS):
                ostage[slot, :, 128 * j : 128 * (j + 1)] = result[PIECE * j : PIECE * (j + 1)]
                cstage[slot, j : j + 1, 0:PIECE] = check[:, PIECE * j : PIECE * (j + 1)]
            copies = out_copy(slot)
            copies[0].start()
            copies[1].start()

        @pl.when(step == 0)
        def _():
            for j in range(HEADS):
                out_ref[:, columns_of(me * HEADS + j, 128)] = result[PIECE * j : PIECE * (j + 1)]
                crecv[me, j : j + 1, 0:PIECE] = check[:, PIECE * j : PIECE * (j + 1)]

        return carry

    lax.fori_loop(0, HEADS, second_half, 0)

    for d in order:
        out_copy(d)[1].wait_recv()
    table = crecv[...].reshape(HEADS * HEADS, 128).T
    chk_out[...] = table[0:PIECE, :]
    for d in order:
        copies = out_copy(d)
        k_copies[d].wait_send()
        v_copies[d].wait_send()
        q_copies[d].wait_send()
        copies[0].wait_send()
        copies[1].wait_send()
    for kind in range(2):
        x_copy(kind).wait_send()
        for line in range(2):
            y_copy(line, 0, kind).wait_send()
            y_copy(line, 1, kind).wait_send()
            f_copy(line, kind).wait_send()
        for slot in range(0, CTX, 2):
            c_copy(slot, kind).wait_send()
    for d in order:
        out_copy(d)[0].wait_recv()


def local(queries, unscaled_key_rows, unscaled_value_rows, key_block_scale, value_block_scale,
          span_order, block_keep):
    vmem = pl.BlockSpec(memory_space=pltpu.VMEM)
    hbm = pl.BlockSpec(memory_space=pltpu.HBM)
    dma = pltpu.SemaphoreType.DMA
    return pl.pallas_call(
        kernel,
        out_shape=(
            jax.ShapeDtypeStruct((PIECE, 8192), jnp.bfloat16),
            jax.ShapeDtypeStruct((PIECE, 64), jnp.float32),
        ),
        in_specs=[hbm] * 7,
        out_specs=(vmem, vmem),
        scratch_shapes=[
            pltpu.SMEM((32,), jnp.float32),
            pltpu.SMEM((32,), jnp.float32),
            pltpu.SMEM((32,), jnp.int32),
            pltpu.SMEM((32, 32), jnp.int32),
            pltpu.SMEM((2, 32), jnp.float32),
            pltpu.SMEM((32,), jnp.float32),
            pltpu.SMEM((32,), jnp.float32),
            pltpu.VMEM((HEADS, PIECE, 1024), jnp.bfloat16),
            pltpu.VMEM((KEYS, HEAD_WIDTH), jnp.bfloat16),
            pltpu.VMEM((KEYS, HEAD_WIDTH), jnp.bfloat16),
            pltpu.VMEM((AUG, KEYS), jnp.bfloat16),
            pltpu.VMEM((HALF, ROWS), jnp.float32),
            pltpu.VMEM((HEADS, AUG, ROWS), jnp.float32),
            pltpu.VMEM((HEADS, 8, ROWS), jnp.float32),
            pltpu.VMEM((HEADS, PIECE, 1024), jnp.bfloat16),
            pltpu.VMEM((HEADS, HEADS, 128), jnp.float32),
            pltpu.VMEM((HEADS, HEADS, 128), jnp.float32),
            dma((4,)),
            dma((3,)),
            dma((2, HEADS)), dma((2, HEADS)),
            dma((HEADS,)), dma((HEADS,)),
            dma((2,)), dma((2,)),
            dma((2, 2, 2)), dma((2, 2, 2)),
            dma((2, 2)), dma((2, 2)),
            dma((8, 2)), dma((8, 2)),
            dma((HEADS,)), dma((HEADS,)),
            dma((HEADS,)), dma((HEADS,)),
        ],
        compiler_params=pltpu.CompilerParams(
            collective_id=0, has_side_effects=True, vmem_limit_bytes=67043328
        ),
    )(
        queries, unscaled_key_rows, unscaled_value_rows,
        key_block_scale.reshape(32), value_block_scale.reshape(32), span_order, block_keep,
    )


def solution(mesh):
    rows = P(("dp", "ctx", "head"), None)
    return jax.shard_map(
        local,
        mesh=mesh,
        in_specs=(rows, rows, rows, P("dp", "head"), P("dp", "head"), P(), P()),
        out_specs=(rows, rows),
        check_vma=False,
    )
```

time: 67.8 us -> 57.7 us (0.85); the launches traced: 66.6 us -> 57.6 us
  Pallas kernels: 60.4 us -> 54.5 us
  local copies, waits for them, and re-layouts: 5.5 us -> 2.48 us
    pallas_call x1, Pallas kernels: 60.4 us -> 54.5 us  [local(): pl.pallas_call(kernel, out_shape=(jax.ShapeDtypeStruct((PIECE, 8192), jnp...]
    unnamed x16 -> x4, local copies, waits for them, and re-layouts: 5.5 us -> 2.48 us
where the time goes in v2:
time: 57.7 us; the launch traced here: 57.6 us
  Pallas kernels  54.5 us (94%)
  local copies, waits for them, and re-layouts  2.48 us (4%)
  between operations  0.65 us (1%)
    pallas_call x1, Pallas kernels, local(): pl.pallas_call(kernel, out_shape=(jax.ShapeDtypeStruct((PIECE, 8192), jnp...  54.5 us
    unnamed x4, local copies, waits for them, and re-layouts  2.48 us

profile of v2, /device:TPU:1, one launch (start us, length us, event | category | flops | bytes accessed | tf_op | source)
XLA Modules:
  0.0 57.6 jit_solution(11407765324031628426)
XLA Ops:
  0.6 54.5 %shard_map.86 = (bf16[32,8192]{1,0:T(8,128)(2,1)}, f32[32,64]{1,0:T(8,128)}) custom-call(bf16[32,8192]{1,0:T(8,128)(2,1)} %q_hbm.1, bf16[32,1024]{1,0:T(8,128)(2,1)} %k_hbm.1, bf16[32,1024]{1,0:T(8,128)(2,1)} %v_hbm.1, f32[32]{0:T(128)} %bitcast.2, f32[32]{0:T(128)} %bitcast.3, s32[32]{0:T(128)} %order_hbm.1, s32[32,32]{1,0:T(8,128)} %keep_hbm.1), custom_call_target="tpu_custom_call" | custom-call | tf_op jit(solution)/shard_map/pallas_call | solution.py:347
  55.1 0.0 copy-start
  55.1 1.9 %copy.11 = bf16[32,8192]{1,0:T(8,128)(2,1)} copy(bf16[32,8192]{1,0:T(8,128)(2,1)} %get-tuple-element.4) | data formatting | bytes 1048576
  57.0 0.0 copy-done
  57.0 0.6 %copy.12 = f32[32,64]{1,0:T(8,128)} copy(f32[32,64]{1,0:T(8,128)S(1)} %copy-done) | data formatting | bytes 16384
Async XLA Ops:
  55.1 1.9 %copy-start = (f32[32,64]{1,0:T(8,128)S(1)}, f32[32,64]{1,0:T(8,128)}, u32[]{:S(2)}) copy-start(f32[32,64]{1,0:T(8,128)} %get-tuple-element.5) | copy-start | bytes 24580

commit v3 on v2

--- a/solution.py
+++ b/solution.py
@@ -28,7 +28,7 @@
     q_hbm, k_hbm, v_hbm, ks_hbm, vs_hbm, order_hbm, keep_hbm,
     out_ref, chk_out,
     ks_ref, vs_ref, order_ref, keep_ref, bias_ref, factor_ref, vfactor_ref,
-    qbuf, kbuf, vbuf, vt, scores, total, peaks, ostage, cstage, crecv,
+    qbuf, kbuf, vbuf, vt, scores_a, scores_b, total, peaks, ostage, cstage, crecv,
     tab_sem, loc_sem, kv_send, kv_recv, q_send, q_recv,
     x_send, x_recv, y_send, y_recv, f_send, f_recv, c_send, c_recv,
     o_send, o_recv, h_send, h_recv,
@@ -174,20 +174,21 @@
     ) | (lax.broadcasted_iota(jnp.int32, (AUG, HEAD_WIDTH), 0) >= HEAD_WIDTH)
     turn = jnp.where(turn, 1.0, 0.0).astype(jnp.bfloat16)
 
-    def turn_values(slot, carry):
-        rows = pl.ds(pl.multiple_of(slot * SHARE, SHARE), SHARE)
-        turned = lax.dot_general(turn, vbuf[rows, :], (((1,), (1,)), ((), ())),
-                                 preferred_element_type=jnp.float32)
-        lane = lax.broadcasted_iota(jnp.int32, (1, SHARE), 1)
-        factor = jnp.where(lane < SPAN, vfactor_ref[2 * slot], vfactor_ref[2 * slot + 1])
-        vt[0:HEAD_WIDTH, rows] = (turned[0:HEAD_WIDTH] * factor).astype(jnp.bfloat16)
-        check = turned[HEAD_WIDTH:AUG] * (factor * INVERSE_ROOT)
-        high = check.astype(jnp.bfloat16).astype(jnp.float32)
-        row = lax.broadcasted_iota(jnp.int32, (16, SHARE), 0)
-        extra = jnp.where(row == 0, 1.0, jnp.where(row == 1, high, jnp.where(row == 2, check - high, 0.0)))
-        vt[HEAD_WIDTH:AUG, rows] = extra.astype(jnp.bfloat16)
-        return carry
-
+    def turn_values(first, last):
+        for slot in range(first, last):
+            rows = rows_of(slot)
+            turned = lax.dot_general(turn, vbuf[rows, :], (((1,), (1,)), ((), ())),
+                                     preferred_element_type=jnp.float32)
+            lane = lax.broadcasted_iota(jnp.int32, (1, SHARE), 1)
+            factor = jnp.where(lane < SPAN, vfactor_ref[2 * slot], vfactor_ref[2 * slot + 1])
+            vt[0:HEAD_WIDTH, rows] = (turned[0:HEAD_WIDTH] * factor).astype(jnp.bfloat16)
+            check = turned[HEAD_WIDTH:AUG] * (factor * INVERSE_ROOT)
+            high = check.astype(jnp.bfloat16).astype(jnp.float32)
+            row = lax.broadcasted_iota(jnp.int32, (16, SHARE), 0)
+            extra = jnp.where(row == 0, 1.0, jnp.where(row == 1, high, jnp.where(row == 2, check - high, 0.0)))
+            vt[HEAD_WIDTH:AUG, rows] = extra.astype(jnp.bfloat16)
+
+    turn_values(0, 1)
     ring_on(0)
     for kind in range(2):
         x_copy(kind).wait_recv()
@@ -196,12 +197,15 @@
         c_copy(8, kind).start()
     ring_end(0)
     from_sibling(0)
-    lax.fori_loop(0, 8, turn_values, 0)
+    turn_values(1, 8)
     own_q.wait()
 
     def slot_of(step):
         half = (step + 1) // 2
         return lax.rem(half * (1 - 2 * lax.rem(step + 1, 2)) + HEADS, HEADS)
+
+    def source_of(slot):
+        return lax.rem(me - slot + HEADS, HEADS)
 
     def load_queries(slot):
         return jnp.concatenate(
@@ -211,7 +215,9 @@
     def block_top(part):
         return jnp.max(part.reshape(SPAN // 8, 8, ROWS), axis=0)
 
-    def score_pass(line, slot, own_half, query_place):
+    def score_unit(line, slot, scores):
+        source = source_of(slot)
+        own_half = source // 4
         query_rows = load_queries(slot)
         highest = jnp.full((8, ROWS), -FAR, jnp.float32)
         for start in range(0, HALF, KEY_CHUNK):
@@ -225,6 +231,9 @@
                 piece = part[i * SPAN : (i + 1) * SPAN]
                 bias = bias_ref[own_half, block]
                 if block < 2:
+                    query_place = PIECE * lax.rem(source, 4) + lax.rem(
+                        lax.broadcasted_iota(jnp.int32, (1, ROWS), 1), PIECE
+                    )
                     free = jnp.where(bias > 0.0, -1, SPAN)
                     limit = jnp.where(own_half == block, query_place, free)
                     key_place = lax.broadcasted_iota(jnp.int32, (SPAN, ROWS), 0)
@@ -232,10 +241,17 @@
                     bias = 0.0
                 scores[start + i * SPAN : start + (i + 1) * SPAN, :] = piece
                 highest = jnp.maximum(highest, block_top(piece) * factor_ref[block] - bias)
-        return jnp.max(highest, axis=0, keepdims=True)
-
-    def value_pass(line, own_half, peak):
-        mixed = jnp.zeros((AUG, ROWS), jnp.float32)
+            yield
+        peak = jnp.max(highest, axis=0, keepdims=True)
+        if line == 1:
+            peak = jnp.maximum(peak, peaks[0, slot, 0:1, :])
+        peaks[line, slot] = jnp.broadcast_to(peak, (8, ROWS))
+
+    def value_unit(line, slot, scores):
+        own_half = source_of(slot) // 4
+        peak = peaks[line, slot, 0:1, :]
+        if line == 1:
+            total[slot] = total[slot] * jnp.exp2(peaks[0, slot, 0:1, :] - peak)
         for start in range(0, HALF, KEY_CHUNK):
             base = line * HALF + start
             weights = []
@@ -244,77 +260,92 @@
                 bias = 0.0 if block < 2 else bias_ref[own_half, block]
                 part = scores[start + i * SPAN : start + (i + 1) * SPAN, :]
                 weights.append(jnp.exp2(part * factor_ref[block] - (peak + bias)).astype(jnp.bfloat16))
-            mixed = mixed + lax.dot_general(
+            product = lax.dot_general(
                 vt[:, base : base + KEY_CHUNK], jnp.concatenate(weights, axis=0),
                 (((1,), (0,)), ((), ())), preferred_element_type=jnp.float32,
             )
-        return mixed
-
-    def place_of_queries(source):
-        return PIECE * lax.rem(source, 4) + lax.rem(lax.broadcasted_iota(jnp.int32, (1, ROWS), 1), PIECE)
-
-    def first_half(step, carry):
-        slot = slot_of(step)
-        source = lax.rem(me - slot + HEADS, HEADS)
-
-        @pl.when(step == 1)
-        def _():
-            ring_on(1)
-
-        @pl.when(step == 4)
-        def _():
-            ring_end(1)
-
-        @pl.when(step > 0)
-        def _():
-            remote(qbuf.at[slot], qbuf.at[slot], q_send.at[slot], q_recv.at[slot], peer(slot)).wait_recv()
-
-        peak = score_pass(0, slot, source // 4, place_of_queries(source))
-        peaks[slot] = jnp.broadcast_to(peak, (8, ROWS))
-        total[slot] = value_pass(0, source // 4, peak)
-        return carry
-
-    lax.fori_loop(0, HEADS, first_half, 0)
-    from_sibling(1)
-    lax.fori_loop(8, CTX, turn_values, 0)
+            if line == 0 and start == 0:
+                total[slot] = product
+            else:
+                total[slot] += product
+            yield
+
+    def finish(slot, own):
+        mixed = total[slot]
+        share = 1.0 / mixed[HEAD_WIDTH : HEAD_WIDTH + 1]
+        result = (mixed[0:HEAD_WIDTH] * share).T.astype(jnp.bfloat16)
+        check = (mixed[HEAD_WIDTH + 1 : HEAD_WIDTH + 2] + mixed[HEAD_WIDTH + 2 : HEAD_WIDTH + 3]) * share
+        for j in range(HEADS):
+            piece = result[PIECE * j : PIECE * (j + 1)]
+            line = check[:, PIECE * j : PIECE * (j + 1)]
+            if own:
+                out_ref[:, columns_of(me * HEADS + j, 128)] = piece
+                crecv[me, j : j + 1, 0:PIECE] = line
+            else:
+                ostage[slot, :, 128 * j : 128 * (j + 1)] = piece
+                cstage[slot, j : j + 1, 0:PIECE] = line
+
+    def run(*units):
+        units = list(units)
+        while units:
+            for unit in list(units):
+                if next(unit, units) is units:
+                    units.remove(unit)
 
     def out_copy(slot):
-        to = {"head": lax.rem(me - slot + HEADS, HEADS)}
+        to = {"head": source_of(slot)}
         return (
             remote(ostage.at[slot], out_ref.at[:, columns_of(me, 1024)],
                    o_send.at[slot], o_recv.at[slot], to),
             remote(cstage.at[slot], crecv.at[me], h_send.at[slot], h_recv.at[slot], to),
         )
 
-    def second_half(back, carry):
-        step = HEADS - 1 - back
+    def queries_here(slot):
+        remote(qbuf.at[slot], qbuf.at[slot], q_send.at[slot], q_recv.at[slot], peer(slot)).wait_recv()
+
+    def first(step, even, odd):
+        after = slot_of(step + 1)
+        queries_here(after)
+        run(value_unit(0, slot_of(step), even), score_unit(0, after, odd))
+
+    def second(step, even, odd):
         slot = slot_of(step)
-        source = lax.rem(me - slot + HEADS, HEADS)
-        first_peak = peaks[slot][0:1]
-        peak = jnp.maximum(first_peak, score_pass(1, slot, source // 4, None))
-        mixed = total[slot] * jnp.exp2(first_peak - peak) + value_pass(1, source // 4, peak)
-        share = 1.0 / mixed[HEAD_WIDTH : HEAD_WIDTH + 1]
-        result = (mixed[0:HEAD_WIDTH] * share).T.astype(jnp.bfloat16)
-        check = (mixed[HEAD_WIDTH + 1 : HEAD_WIDTH + 2] + mixed[HEAD_WIDTH + 2 : HEAD_WIDTH + 3]) * share
-
-        @pl.when(step > 0)
+        run(value_unit(1, slot, even), score_unit(1, slot_of(step - 1), odd))
+        finish(slot, False)
+        copies = out_copy(slot)
+        copies[0].start()
+        copies[1].start()
+
+    run(score_unit(0, 0, scores_a))
+
+    def first_pair(pair, carry):
+        @pl.when(pair == 1)
         def _():
-            for j in range(HEADS):
-                ostage[slot, :, 128 * j : 128 * (j + 1)] = result[PIECE * j : PIECE * (j + 1)]
-                cstage[slot, j : j + 1, 0:PIECE] = check[:, PIECE * j : PIECE * (j + 1)]
-            copies = out_copy(slot)
-            copies[0].start()
-            copies[1].start()
-
-        @pl.when(step == 0)
+            ring_on(1)
+
+        @pl.when(pair == 2)
         def _():
-            for j in range(HEADS):
-                out_ref[:, columns_of(me * HEADS + j, 128)] = result[PIECE * j : PIECE * (j + 1)]
-                crecv[me, j : j + 1, 0:PIECE] = check[:, PIECE * j : PIECE * (j + 1)]
-
+            ring_end(1)
+
+        first(2 * pair, scores_a, scores_b)
+        first(2 * pair + 1, scores_b, scores_a)
         return carry
 
-    lax.fori_loop(0, HEADS, second_half, 0)
+    lax.fori_loop(0, 3, first_pair, 0)
+    first(6, scores_a, scores_b)
+    from_sibling(1)
+    turn_values(8, CTX)
+    run(value_unit(0, slot_of(7), scores_b), score_unit(1, slot_of(7), scores_a))
+
+    def second_pair(pair, carry):
+        second(7 - 2 * pair, scores_a, scores_b)
+        second(6 - 2 * pair, scores_b, scores_a)
+        return carry
+
+    lax.fori_loop(0, 3, second_pair, 0)
+    second(1, scores_a, scores_b)
+    run(value_unit(1, 0, scores_b))
+    finish(0, True)
 
     for d in order:
         out_copy(d)[1].wait_recv()
@@ -365,8 +396,9 @@
             pltpu.VMEM((KEYS, HEAD_WIDTH), jnp.bfloat16),
             pltpu.VMEM((AUG, KEYS), jnp.bfloat16),
             pltpu.VMEM((HALF, ROWS), jnp.float32),
+            pltpu.VMEM((HALF, ROWS), jnp.float32),
             pltpu.VMEM((HEADS, AUG, ROWS), jnp.float32),
-            pltpu.VMEM((HEADS, 8, ROWS), jnp.float32),
+            pltpu.VMEM((2, HEADS, 8, ROWS), jnp.float32),
             pltpu.VMEM((HEADS, PIECE, 1024), jnp.bfloat16),
             pltpu.VMEM((HEADS, HEADS, 128), jnp.float32),
             pltpu.VMEM((HEADS, HEADS, 128), jnp.float32),

time: 57.7 us -> 53.6 us (0.929)
  Pallas kernels: 54.5 us -> 50.3 us
    pallas_call x1, Pallas kernels: 54.5 us -> 50.3 us  [local(): pl.pallas_call(kernel, out_shape=(jax.ShapeDtypeStruct((PIECE, 8192), jnp...]
where the time goes in v3:
time: 53.6 us; the launch traced here: 53.5 us
  Pallas kernels  50.3 us (94%)
  local copies, waits for them, and re-layouts  2.48 us (5%)
  between operations  0.65 us (1%)
    pallas_call x1, Pallas kernels, local(): pl.pallas_call(kernel, out_shape=(jax.ShapeDtypeStruct((PIECE, 8192), jnp...  50.3 us
    unnamed x4, local copies, waits for them, and re-layouts  2.48 us

profile of v3, /device:TPU:1, one launch (start us, length us, event | category | flops | bytes accessed | tf_op | source)
XLA Modules:
  0.0 53.5 jit_solution(15744566590854213813)
XLA Ops:
  0.6 50.3 %shard_map.86 = (bf16[32,8192]{1,0:T(8,128)(2,1)}, f32[32,64]{1,0:T(8,128)}) custom-call(bf16[32,8192]{1,0:T(8,128)(2,1)} %q_hbm.1, bf16[32,1024]{1,0:T(8,128)(2,1)} %k_hbm.1, bf16[32,1024]{1,0:T(8,128)(2,1)} %v_hbm.1, f32[32]{0:T(128)} %bitcast.2, f32[32]{0:T(128)} %bitcast.3, s32[32]{0:T(128)} %order_hbm.1, s32[32,32]{1,0:T(8,128)} %keep_hbm.1), custom_call_target="tpu_custom_call" | custom-call | tf_op jit(solution)/shard_map/pallas_call | solution.py:378
  51.0 0.0 copy-start
  51.0 1.9 %copy.11 = bf16[32,8192]{1,0:T(8,128)(2,1)} copy(bf16[32,8192]{1,0:T(8,128)(2,1)} %get-tuple-element.4) | data formatting | bytes 1048576
  52.8 0.0 copy-done
  52.8 0.6 %copy.12 = f32[32,64]{1,0:T(8,128)} copy(f32[32,64]{1,0:T(8,128)S(1)} %copy-done) | data formatting | bytes 16384
Async XLA Ops:
  51.0 1.9 %copy-start = (f32[32,64]{1,0:T(8,128)S(1)}, f32[32,64]{1,0:T(8,128)}, u32[]{:S(2)}) copy-start(f32[32,64]{1,0:T(8,128)} %get-tuple-element.5) | copy-start | bytes 24580

commit v4 on v3

--- a/solution.py
+++ b/solution.py
@@ -98,6 +98,7 @@
         q_copies[d].start()
 
     bufs = (kbuf, vbuf)
+    where = {(0, 0): 0, (0, 1): 2, (0, 2): 4, (1, 0): 6, (0, 3): 8, (1, 1): 10, (1, 2): 12, (1, 3): 14}
 
     def rows_of(slot):
         return pl.ds(slot * SHARE, SHARE)
@@ -106,14 +107,14 @@
         return remote(bufs[kind].at[rows_of(slot)], bufs[kind].at[rows_of(to_slot)], send, recv, device)
 
     def x_copy(kind):
-        return ship(kind, 0, 8, x_send.at[kind], x_recv.at[kind], across)
+        return ship(kind, 0, where[1, 0], x_send.at[kind], x_recv.at[kind], across)
 
     def y_copy(line, way, kind):
-        return ship(kind, 8 * line, 8 * line + 2 + 2 * way, y_send.at[line, way, kind],
+        return ship(kind, where[line, 0], where[line, 1 + way], y_send.at[line, way, kind],
                     y_recv.at[line, way, kind], (up, down)[way])
 
     def f_copy(line, kind):
-        return ship(kind, 8 * line + 2 + 2 * kind, 8 * line + 6, f_send.at[line, kind],
+        return ship(kind, where[line, 1 + kind], where[line, 3], f_send.at[line, kind],
                     f_recv.at[line, kind], (up, down)[kind])
 
     def c_copy(slot, kind):
@@ -136,9 +137,9 @@
 
     for copy in tables:
         copy.wait()
-    for slot in range(CTX):
-        at = place(ys[slot % 8 // 2], xh if slot < 8 else 1 - xh, core if slot % 2 == 0 else 1 - core)
-        for i in range(2):
+    for (line, way), even in where.items():
+        for slot, i in ((even, 0), (even, 1), (even + 1, 0), (even + 1, 1)):
+            at = place(ys[way], xh if line == 0 else 1 - xh, core if slot == even else 1 - core)
             block = 2 * at + i
             factor_ref[2 * slot + i] = ks_ref[block] * SCORE_FACTOR
             vfactor_ref[2 * slot + i] = vs_ref[block]
@@ -146,25 +147,8 @@
                 seen = (keep_ref[2 * ctx + q, block] > 0) & (order_ref[2 * ctx + q] > order_ref[block])
                 bias_ref[q, 2 * slot + i] = jnp.where(seen, jnp.float32(0.0), jnp.float32(FAR))
 
-    def ring_on(line):
-        y_copy(line, 0, 0).wait_recv()
-        f_copy(line, 0).start()
-        y_copy(line, 1, 1).wait_recv()
-        f_copy(line, 1).start()
-        c_copy(8 * line + 2, 0).start()
-        c_copy(8 * line + 4, 1).start()
-        y_copy(line, 1, 0).wait_recv()
-        c_copy(8 * line + 4, 0).start()
-        y_copy(line, 0, 1).wait_recv()
-        c_copy(8 * line + 2, 1).start()
-
-    def ring_end(line):
-        for kind in range(2):
-            f_copy(line, kind).wait_recv()
-            c_copy(8 * line + 6, kind).start()
-
-    def from_sibling(line):
-        for slot in range(8 * line, 8 * line + 8, 2):
+    def from_sibling(*slots):
+        for slot in slots:
             for kind in range(2):
                 c_copy(slot, kind).wait_recv()
 
@@ -174,8 +158,8 @@
     ) | (lax.broadcasted_iota(jnp.int32, (AUG, HEAD_WIDTH), 0) >= HEAD_WIDTH)
     turn = jnp.where(turn, 1.0, 0.0).astype(jnp.bfloat16)
 
-    def turn_values(first, last):
-        for slot in range(first, last):
+    def turn_unit(*slots):
+        for slot in slots:
             rows = rows_of(slot)
             turned = lax.dot_general(turn, vbuf[rows, :], (((1,), (1,)), ((), ())),
                                      preferred_element_type=jnp.float32)
@@ -187,17 +171,43 @@
             row = lax.broadcasted_iota(jnp.int32, (16, SHARE), 0)
             extra = jnp.where(row == 0, 1.0, jnp.where(row == 1, high, jnp.where(row == 2, check - high, 0.0)))
             vt[HEAD_WIDTH:AUG, rows] = extra.astype(jnp.bfloat16)
-
-    turn_values(0, 1)
-    ring_on(0)
-    for kind in range(2):
-        x_copy(kind).wait_recv()
-        y_copy(1, kind, kind).start()
-        y_copy(1, 1 - kind, kind).start()
-        c_copy(8, kind).start()
-    ring_end(0)
-    from_sibling(0)
-    turn_values(1, 8)
+            yield
+
+    def run(*units):
+        units = list(units)
+        while units:
+            for unit in list(units):
+                if next(unit, units) is units:
+                    units.remove(unit)
+
+    run(turn_unit(0))
+    y_copy(0, 0, 0).wait_recv()
+    f_copy(0, 0).start()
+    c_copy(2, 0).start()
+    y_copy(0, 1, 0).wait_recv()
+    c_copy(4, 0).start()
+    x_copy(0).wait_recv()
+    y_copy(1, 0, 0).start()
+    y_copy(1, 1, 0).start()
+    c_copy(6, 0).start()
+    y_copy(0, 1, 1).wait_recv()
+    f_copy(0, 1).start()
+    c_copy(4, 1).start()
+    y_copy(0, 0, 1).wait_recv()
+    c_copy(2, 1).start()
+    x_copy(1).wait_recv()
+    y_copy(1, 1, 1).start()
+    y_copy(1, 0, 1).start()
+    c_copy(6, 1).start()
+    f_copy(0, 0).wait_recv()
+    c_copy(8, 0).start()
+    y_copy(1, 0, 0).wait_recv()
+    f_copy(1, 0).start()
+    c_copy(10, 0).start()
+    y_copy(1, 1, 0).wait_recv()
+    c_copy(12, 0).start()
+    run(turn_unit(2, 4, 6))
+    from_sibling(0, 2, 4, 6)
     own_q.wait()
 
     def slot_of(step):
@@ -285,13 +295,6 @@
                 ostage[slot, :, 128 * j : 128 * (j + 1)] = piece
                 cstage[slot, j : j + 1, 0:PIECE] = line
 
-    def run(*units):
-        units = list(units)
-        while units:
-            for unit in list(units):
-                if next(unit, units) is units:
-                    units.remove(unit)
-
     def out_copy(slot):
         to = {"head": source_of(slot)}
         return (
@@ -303,10 +306,10 @@
     def queries_here(slot):
         remote(qbuf.at[slot], qbuf.at[slot], q_send.at[slot], q_recv.at[slot], peer(slot)).wait_recv()
 
-    def first(step, even, odd):
+    def first(step, even, odd, *more):
         after = slot_of(step + 1)
         queries_here(after)
-        run(value_unit(0, slot_of(step), even), score_unit(0, after, odd))
+        run(value_unit(0, slot_of(step), even), score_unit(0, after, odd), *more)
 
     def second(step, even, odd):
         slot = slot_of(step)
@@ -316,26 +319,38 @@
         copies[0].start()
         copies[1].start()
 
-    run(score_unit(0, 0, scores_a))
+    run(score_unit(0, 0, scores_a), turn_unit(1, 3, 5, 7))
 
     def first_pair(pair, carry):
+        @pl.when(pair == 0)
+        def _():
+            f_copy(0, 1).wait_recv()
+            c_copy(8, 1).start()
+            y_copy(1, 1, 1).wait_recv()
+            f_copy(1, 1).start()
+            c_copy(12, 1).start()
+            y_copy(1, 0, 1).wait_recv()
+            c_copy(10, 1).start()
+
         @pl.when(pair == 1)
         def _():
-            ring_on(1)
+            f_copy(1, 0).wait_recv()
+            c_copy(14, 0).start()
 
         @pl.when(pair == 2)
         def _():
-            ring_end(1)
+            f_copy(1, 1).wait_recv()
+            c_copy(14, 1).start()
 
         first(2 * pair, scores_a, scores_b)
         first(2 * pair + 1, scores_b, scores_a)
         return carry
 
     lax.fori_loop(0, 3, first_pair, 0)
-    first(6, scores_a, scores_b)
-    from_sibling(1)
-    turn_values(8, CTX)
-    run(value_unit(0, slot_of(7), scores_b), score_unit(1, slot_of(7), scores_a))
+    from_sibling(8, 10, 12)
+    first(6, scores_a, scores_b, turn_unit(8, 9, 10, 11, 12, 13))
+    from_sibling(14)
+    run(value_unit(0, slot_of(7), scores_b), score_unit(1, slot_of(7), scores_a), turn_unit(14, 15))
 
     def second_pair(pair, carry):
         second(7 - 2 * pair, scores_a, scores_b)
@@ -414,12 +429,15 @@
             dma((HEADS,)), dma((HEADS,)),
         ],
         compiler_params=pltpu.CompilerParams(
-            collective_id=0, has_side_effects=True, vmem_limit_bytes=67043328
+            collective_id=0, has_side_effects=True, vmem_limit_bytes=40 << 20
         ),
-    )(
-        queries, unscaled_key_rows, unscaled_value_rows,
-        key_block_scale.reshape(32), value_block_scale.reshape(32), span_order, block_keep,
-    )
+    )(*(
+        pltpu.with_memory_space_constraint(operand, pltpu.HBM)
+        for operand in (
+            queries, unscaled_key_rows, unscaled_value_rows,
+            key_block_scale.reshape(32), value_block_scale.reshape(32), span_order, block_keep,
+        )
+    ))
 
 
 def solution(mesh):

time: 53.6 us -> 50 us (0.933)
  Pallas kernels: 50.3 us -> 47.9 us
  local copies, waits for them, and re-layouts: 2.48 us -> 1.4 us
    pallas_call x1, Pallas kernels: 50.3 us -> 47.9 us  [local(): pl.pallas_call(kernel, out_shape=(jax.ShapeDtypeStruct((PIECE, 8192), jnp...]
    unnamed x4 -> x2, local copies, waits for them, and re-layouts: 2.48 us -> 1.4 us
where the time goes in v4:
time: 50 us; the launch traced here: 49.9 us
  Pallas kernels  47.9 us (96%)
  local copies, waits for them, and re-layouts  1.4 us (3%)
  between operations  0.64 us (1%)
    pallas_call x1, Pallas kernels, local(): pl.pallas_call(kernel, out_shape=(jax.ShapeDtypeStruct((PIECE, 8192), jnp...  47.9 us
    unnamed x2, local copies, waits for them, and re-layouts  1.4 us

profile of v4, /device:TPU:1, one launch (start us, length us, event | category | flops | bytes accessed | tf_op | source)
XLA Modules:
  0.0 49.9 jit_solution(12306135954028690059)
XLA Ops:
  0.6 47.9 %shard_map.86 = (bf16[32,8192]{1,0:T(8,128)(2,1)S(1)}, f32[32,64]{1,0:T(8,128)S(1)}) custom-call(bf16[32,8192]{1,0:T(8,128)(2,1)} %q_hbm.1, bf16[32,1024]{1,0:T(8,128)(2,1)} %k_hbm.1, bf16[32,1024]{1,0:T(8,128)(2,1)} %v_hbm.1, f32[32]{0:T(128)} %bitcast.2, f32[32]{0:T(128)} %bitcast.3, s32[32]{0:T(128)} %order_hbm.1, s32[32,32]{1,0:T(8,128)} %keep_hbm.1), custom_call_target="tpu_custom_call" | custom-call | tf_op jit(solution)/shard_map/pallas_call | solution.py:393
  48.5 0.8 %copy.11 = bf16[32,8192]{1,0:T(8,128)(2,1)} copy(bf16[32,8192]{1,0:T(8,128)(2,1)S(1)} %get-tuple-element.4) | data formatting | bytes 1048576
  49.3 0.6 %copy.12 = f32[32,64]{1,0:T(8,128)} copy(f32[32,64]{1,0:T(8,128)S(1)} %get-tuple-element.5) | data formatting | bytes 16384

commit v5 on v4

--- a/solution.py
+++ b/solution.py
@@ -19,7 +19,7 @@
 FAR = 1e30
 INVERSE_ROOT = 1.0 / math.sqrt(HEAD_WIDTH)
 SCORE_FACTOR = INVERSE_ROOT * 1.4426950408889634
-HALF = KEYS // 2
+GROUPS = ((0, 4 * SHARE), (4 * SHARE, KEYS))
 KEY_CHUNK = 512
 MESH = pl.DeviceIdType.MESH
 
@@ -29,9 +29,8 @@
     out_ref, chk_out,
     ks_ref, vs_ref, order_ref, keep_ref, bias_ref, factor_ref, vfactor_ref,
     qbuf, kbuf, vbuf, vt, scores_a, scores_b, total, peaks, ostage, cstage, crecv,
-    tab_sem, loc_sem, kv_send, kv_recv, q_send, q_recv,
-    x_send, x_recv, y_send, y_recv, f_send, f_recv, c_send, c_recv,
-    o_send, o_recv, h_send, h_recv,
+    tab_sem, loc_sem, kv_send, kv_recv, q_send, q_recv, g_send, x_recv, y_recv, f_recv, c_recv, d_recv,
+    o_send, o_recv,
 ):
     ctx = lax.axis_index("ctx")
     me = lax.axis_index("head")
@@ -47,6 +46,7 @@
     down = {"ctx": place(ys[1], xh, core)}
     across = {"ctx": place(y, 1 - xh, core)}
     sibling = {"ctx": place(y, xh, 1 - core)}
+    opposite = {"ctx": place(ys[3], xh, core)}
 
     def peer(d):
         return {"head": lax.rem(me + d, HEADS)}
@@ -60,7 +60,7 @@
     barrier = pltpu.get_barrier_semaphore()
     for d in range(1, HEADS):
         pl.semaphore_signal(barrier, inc=1, device_id=peer(d), device_id_type=MESH)
-    for device in (up, down, across, sibling):
+    for device in (up, down, across, sibling, opposite):
         pl.semaphore_signal(barrier, inc=1, device_id=device, device_id_type=MESH)
 
     def columns_of(group, width):
@@ -78,18 +78,18 @@
     own_q = pltpu.make_async_copy(q_hbm.at[:, columns_of(me, 1024)], qbuf.at[0], loc_sem.at[2])
     for copy in tables + [own_k, own_v, own_q]:
         copy.start()
-    pl.semaphore_wait(barrier, HEADS - 1 + 4)
+    pl.semaphore_wait(barrier, HEADS - 1 + 5)
 
     order = [1, 7, 2, 6, 3, 5, 4]
     k_copies, v_copies, q_copies = {}, {}, {}
     for d in range(1, HEADS):
         to = lax.rem(me + d, HEADS)
         k_copies[d] = remote(k_hbm.at[:, columns_of(to, 128)], kbuf.at[landing],
-                             kv_send.at[0, d], kv_recv.at[0, d], peer(d))
+                             kv_send.at[0], kv_recv.at[0], peer(d))
         v_copies[d] = remote(v_hbm.at[:, columns_of(to, 128)], vbuf.at[landing],
-                             kv_send.at[1, d], kv_recv.at[1, d], peer(d))
+                             kv_send.at[1], kv_recv.at[1], peer(d))
         q_copies[d] = remote(q_hbm.at[:, columns_of(to, 1024)], qbuf.at[d],
-                             q_send.at[d], q_recv.at[d], peer(d))
+                             q_send, q_recv.at[d], peer(d))
     for d in reversed(order):
         k_copies[d].start()
     for d in reversed(order):
@@ -98,7 +98,8 @@
         q_copies[d].start()
 
     bufs = (kbuf, vbuf)
-    where = {(0, 0): 0, (0, 1): 2, (0, 2): 4, (1, 0): 6, (0, 3): 8, (1, 1): 10, (1, 2): 12, (1, 3): 14}
+    where = {(0, 0): 0, (0, 1): 2, (0, 2): 3, (1, 0): 6, (0, 3): 8, (1, 1): 10, (1, 2): 12, (1, 3): 14}
+    twin = {0: 1, 2: 4, 3: 5, 6: 7, 8: 9, 10: 11, 12: 13, 14: 15}
 
     def rows_of(slot):
         return pl.ds(slot * SHARE, SHARE)
@@ -107,29 +108,35 @@
         return remote(bufs[kind].at[rows_of(slot)], bufs[kind].at[rows_of(to_slot)], send, recv, device)
 
     def x_copy(kind):
-        return ship(kind, 0, where[1, 0], x_send.at[kind], x_recv.at[kind], across)
+        return ship(kind, 0, where[1, 0], g_send.at[kind], x_recv.at[kind], across)
 
     def y_copy(line, way, kind):
-        return ship(kind, where[line, 0], where[line, 1 + way], y_send.at[line, way, kind],
+        return ship(kind, where[line, 0], where[line, 1 + way], g_send.at[kind],
                     y_recv.at[line, way, kind], (up, down)[way])
 
-    def f_copy(line, kind):
-        return ship(kind, where[line, 1 + kind], where[line, 3], f_send.at[line, kind],
-                    f_recv.at[line, kind], (up, down)[kind])
+    def f_copy(kind):
+        return ship(kind, where[0, 1 + kind], where[0, 3], g_send.at[kind], f_recv.at[kind],
+                    (up, down)[kind])
+
+    def d_copy(kind):
+        return ship(kind, where[1, 0], where[1, 3], g_send.at[kind], d_recv.at[kind], opposite)
 
     def c_copy(slot, kind):
-        return ship(kind, slot, slot + 1, c_send.at[slot // 2, kind], c_recv.at[slot // 2, kind], sibling)
+        return ship(kind, slot, twin[slot], g_send.at[kind], c_recv.at[slot // 2 if slot != 3 else 2, kind], sibling)
 
     own_k.wait()
-    for d in order:
-        k_copies[d].wait_recv()
+    pieces = pl.ds(0, (HEADS - 1) * PIECE)
+
+    def await_bytes(ref, sem):
+        pltpu.make_async_copy(ref, ref, sem).wait()
+
+    await_bytes(kbuf.at[pieces], kv_recv.at[0])
     x_copy(0).start()
     y_copy(0, 0, 0).start()
     y_copy(0, 1, 0).start()
     c_copy(0, 0).start()
     own_v.wait()
-    for d in order:
-        v_copies[d].wait_recv()
+    await_bytes(vbuf.at[pieces], kv_recv.at[1])
     x_copy(1).start()
     y_copy(0, 1, 1).start()
     y_copy(0, 0, 1).start()
@@ -138,7 +145,7 @@
     for copy in tables:
         copy.wait()
     for (line, way), even in where.items():
-        for slot, i in ((even, 0), (even, 1), (even + 1, 0), (even + 1, 1)):
+        for slot, i in ((even, 0), (even, 1), (twin[even], 0), (twin[even], 1)):
             at = place(ys[way], xh if line == 0 else 1 - xh, core if slot == even else 1 - core)
             block = 2 * at + i
             factor_ref[2 * slot + i] = ks_ref[block] * SCORE_FACTOR
@@ -182,32 +189,27 @@
 
     run(turn_unit(0))
     y_copy(0, 0, 0).wait_recv()
-    f_copy(0, 0).start()
+    f_copy(0).start()
     c_copy(2, 0).start()
     y_copy(0, 1, 0).wait_recv()
-    c_copy(4, 0).start()
+    c_copy(3, 0).start()
     x_copy(0).wait_recv()
+    d_copy(0).start()
     y_copy(1, 0, 0).start()
     y_copy(1, 1, 0).start()
     c_copy(6, 0).start()
     y_copy(0, 1, 1).wait_recv()
-    f_copy(0, 1).start()
-    c_copy(4, 1).start()
+    f_copy(1).start()
+    c_copy(3, 1).start()
     y_copy(0, 0, 1).wait_recv()
     c_copy(2, 1).start()
     x_copy(1).wait_recv()
+    d_copy(1).start()
     y_copy(1, 1, 1).start()
     y_copy(1, 0, 1).start()
     c_copy(6, 1).start()
-    f_copy(0, 0).wait_recv()
-    c_copy(8, 0).start()
-    y_copy(1, 0, 0).wait_recv()
-    f_copy(1, 0).start()
-    c_copy(10, 0).start()
-    y_copy(1, 1, 0).wait_recv()
-    c_copy(12, 0).start()
-    run(turn_unit(2, 4, 6))
-    from_sibling(0, 2, 4, 6)
+    run(turn_unit(2, 3))
+    from_sibling(0)
     own_q.wait()
 
     def slot_of(step):
@@ -230,8 +232,8 @@
         own_half = source // 4
         query_rows = load_queries(slot)
         highest = jnp.full((8, ROWS), -FAR, jnp.float32)
-        for start in range(0, HALF, KEY_CHUNK):
-            base = line * HALF + start
+        for base in range(*GROUPS[line], KEY_CHUNK):
+            start = base - GROUPS[line][0]
             part = lax.dot_general(
                 kbuf[base : base + KEY_CHUNK, :], query_rows, (((1,), (1,)), ((), ())),
                 preferred_element_type=jnp.float32,
@@ -262,8 +264,8 @@
         peak = peaks[line, slot, 0:1, :]
         if line == 1:
             total[slot] = total[slot] * jnp.exp2(peaks[0, slot, 0:1, :] - peak)
-        for start in range(0, HALF, KEY_CHUNK):
-            base = line * HALF + start
+        for base in range(*GROUPS[line], KEY_CHUNK):
+            start = base - GROUPS[line][0]
             weights = []
             for i in range(KEY_CHUNK // SPAN):
                 block = base // SPAN + i
@@ -299,12 +301,12 @@
         to = {"head": source_of(slot)}
         return (
             remote(ostage.at[slot], out_ref.at[:, columns_of(me, 1024)],
-                   o_send.at[slot], o_recv.at[slot], to),
-            remote(cstage.at[slot], crecv.at[me], h_send.at[slot], h_recv.at[slot], to),
+                   o_send.at[0], o_recv.at[0], to),
+            remote(cstage.at[slot], crecv.at[me], o_send.at[1], o_recv.at[1], to),
         )
 
     def queries_here(slot):
-        remote(qbuf.at[slot], qbuf.at[slot], q_send.at[slot], q_recv.at[slot], peer(slot)).wait_recv()
+        remote(qbuf.at[slot], qbuf.at[slot], q_send, q_recv.at[slot], peer(slot)).wait_recv()
 
     def first(step, even, odd, *more):
         after = slot_of(step + 1)
@@ -319,38 +321,42 @@
         copies[0].start()
         copies[1].start()
 
-    run(score_unit(0, 0, scores_a), turn_unit(1, 3, 5, 7))
+    run(score_unit(0, 0, scores_a), turn_unit(1))
+
+    def line_one(kind):
+        y_copy(1, 0, kind).wait_recv()
+        c_copy(10, kind).start()
+        y_copy(1, 1, kind).wait_recv()
+        c_copy(12, kind).start()
+        d_copy(kind).wait_recv()
+        c_copy(14, kind).start()
 
     def first_pair(pair, carry):
         @pl.when(pair == 0)
         def _():
-            f_copy(0, 1).wait_recv()
-            c_copy(8, 1).start()
-            y_copy(1, 1, 1).wait_recv()
-            f_copy(1, 1).start()
-            c_copy(12, 1).start()
-            y_copy(1, 0, 1).wait_recv()
-            c_copy(10, 1).start()
+            f_copy(0).wait_recv()
+            c_copy(8, 0).start()
 
         @pl.when(pair == 1)
         def _():
-            f_copy(1, 0).wait_recv()
-            c_copy(14, 0).start()
+            line_one(0)
+            f_copy(1).wait_recv()
+            c_copy(8, 1).start()
 
         @pl.when(pair == 2)
         def _():
-            f_copy(1, 1).wait_recv()
-            c_copy(14, 1).start()
+            line_one(1)
 
         first(2 * pair, scores_a, scores_b)
         first(2 * pair + 1, scores_b, scores_a)
         return carry
 
     lax.fori_loop(0, 3, first_pair, 0)
-    from_sibling(8, 10, 12)
-    first(6, scores_a, scores_b, turn_unit(8, 9, 10, 11, 12, 13))
-    from_sibling(14)
-    run(value_unit(0, slot_of(7), scores_b), score_unit(1, slot_of(7), scores_a), turn_unit(14, 15))
+    from_sibling(2, 3, 6)
+    first(6, scores_a, scores_b, turn_unit(4, 5, 6, 7))
+    from_sibling(8, 10, 12, 14)
+    run(value_unit(0, slot_of(7), scores_b), score_unit(1, slot_of(7), scores_a),
+        turn_unit(*range(8, CTX)))
 
     def second_pair(pair, carry):
         second(7 - 2 * pair, scores_a, scores_b)
@@ -362,27 +368,28 @@
     run(value_unit(1, 0, scores_b))
     finish(0, True)
 
-    for d in order:
-        out_copy(d)[1].wait_recv()
+    await_bytes(cstage.at[1:], o_recv.at[1])
     table = crecv[...].reshape(HEADS * HEADS, 128).T
     chk_out[...] = table[0:PIECE, :]
-    for d in order:
-        copies = out_copy(d)
-        k_copies[d].wait_send()
-        v_copies[d].wait_send()
-        q_copies[d].wait_send()
-        copies[0].wait_send()
-        copies[1].wait_send()
+    await_bytes(kbuf.at[pieces], kv_send.at[0])
+    await_bytes(vbuf.at[pieces], kv_send.at[1])
+    await_bytes(qbuf.at[1:], q_send)
     for kind in range(2):
-        x_copy(kind).wait_send()
-        for line in range(2):
-            y_copy(line, 0, kind).wait_send()
-            y_copy(line, 1, kind).wait_send()
-            f_copy(line, kind).wait_send()
-        for slot in range(0, CTX, 2):
-            c_copy(slot, kind).wait_send()
-    for d in order:
-        out_copy(d)[0].wait_recv()
+        await_bytes(bufs[kind].at[0 : 15 * SHARE], g_send.at[kind])
+    await_bytes(cstage.at[1:], o_send.at[1])
+    await_bytes(ostage.at[1:], o_send.at[0])
+    await_bytes(ostage.at[1:], o_recv.at[0])
+
+
+def put(rows_in, checks_in, rows_out, checks_out, sems):
+    copies = [
+        pltpu.make_async_copy(rows_in, rows_out, sems.at[0]),
+        pltpu.make_async_copy(checks_in, checks_out, sems.at[1]),
+    ]
+    for copy in copies:
+        copy.start()
+    for copy in copies:
+        copy.wait()
 
 
 def local(queries, unscaled_key_rows, unscaled_value_rows, key_block_scale, value_block_scale,
@@ -390,7 +397,7 @@
     vmem = pl.BlockSpec(memory_space=pltpu.VMEM)
     hbm = pl.BlockSpec(memory_space=pltpu.HBM)
     dma = pltpu.SemaphoreType.DMA
-    return pl.pallas_call(
+    attended, checks = pl.pallas_call(
         kernel,
         out_shape=(
             jax.ShapeDtypeStruct((PIECE, 8192), jnp.bfloat16),
@@ -410,8 +417,8 @@
             pltpu.VMEM((KEYS, HEAD_WIDTH), jnp.bfloat16),
             pltpu.VMEM((KEYS, HEAD_WIDTH), jnp.bfloat16),
             pltpu.VMEM((AUG, KEYS), jnp.bfloat16),
-            pltpu.VMEM((HALF, ROWS), jnp.float32),
-            pltpu.VMEM((HALF, ROWS), jnp.float32),
+            pltpu.VMEM((KEYS - GROUPS[1][0], ROWS), jnp.float32),
+            pltpu.VMEM((KEYS - GROUPS[1][0], ROWS), jnp.float32),
             pltpu.VMEM((HEADS, AUG, ROWS), jnp.float32),
             pltpu.VMEM((2, HEADS, 8, ROWS), jnp.float32),
             pltpu.VMEM((HEADS, PIECE, 1024), jnp.bfloat16),
@@ -419,14 +426,10 @@
             pltpu.VMEM((HEADS, HEADS, 128), jnp.float32),
             dma((4,)),
             dma((3,)),
-            dma((2, HEADS)), dma((2, HEADS)),
-            dma((HEADS,)), dma((HEADS,)),
             dma((2,)), dma((2,)),
-            dma((2, 2, 2)), dma((2, 2, 2)),
-            dma((2, 2)), dma((2, 2)),
-            dma((8, 2)), dma((8, 2)),
-            dma((HEADS,)), dma((HEADS,)),
-            dma((HEADS,)), dma((HEADS,)),
+            dma, dma((HEADS,)),
+            dma((2,)), dma((2,)), dma((2, 2, 2)), dma((2,)), dma((8, 2)), dma((2,)),
+            dma((2,)), dma((2,)),
         ],
         compiler_params=pltpu.CompilerParams(
             collective_id=0, has_side_effects=True, vmem_limit_bytes=40 << 20
@@ -438,6 +441,17 @@
             key_block_scale.reshape(32), value_block_scale.reshape(32), span_order, block_keep,
         )
     ))
+    return pl.pallas_call(
+        put,
+        out_shape=(
+            jax.ShapeDtypeStruct((PIECE, 8192), jnp.bfloat16),
+            jax.ShapeDtypeStruct((PIECE, 64), jnp.float32),
+        ),
+        in_specs=[vmem, vmem],
+        out_specs=(hbm, hbm),
+        scratch_shapes=[dma((2,))],
+        compiler_params=pltpu.CompilerParams(vmem_limit_bytes=1 << 20),
+    )(attended, checks)
 
 
 def solution(mesh):

time: 50 us -> 47.1 us (0.942)
  Pallas kernels: 47.9 us -> 46.4 us
  local copies, waits for them, and re-layouts: 1.4 us -> 0 us
    pallas_call x1, Pallas kernels: 47.9 us -> 45.6 us  [local(): pl.pallas_call(kernel, out_shape=(jax.ShapeDtypeStruct((PIECE, 8192), jnp...]
    unnamed x2 -> x0, local copies, waits for them, and re-layouts: 1.4 us -> none
    pallas_call x0 -> x1, Pallas kernels: none -> 0.81 us  [local(): pl.pallas_call(put, out_shape=(jax.ShapeDtypeStruct((PIECE, 8192), jnp.bf...]
where the time goes in v5:
time: 47.1 us; the launch traced here: 47 us
  Pallas kernels  46.4 us (99%)
  between operations  0.64 us (1%)
    pallas_call x1, Pallas kernels, local(): pl.pallas_call(kernel, out_shape=(jax.ShapeDtypeStruct((PIECE, 8192), jnp...  45.6 us

profile of v5, /device:TPU:1, one launch (start us, length us, event | category | flops | bytes accessed | tf_op | source)
XLA Modules:
  0.0 47.0 jit_solution(4526137134934463839)
XLA Ops:
  0.6 45.6 %shard_map.86 = (bf16[32,8192]{1,0:T(8,128)(2,1)S(1)}, f32[32,64]{1,0:T(8,128)S(1)}) custom-call(bf16[32,8192]{1,0:T(8,128)(2,1)} %q_hbm.1, bf16[32,1024]{1,0:T(8,128)(2,1)} %k_hbm.1, bf16[32,1024]{1,0:T(8,128)(2,1)} %v_hbm.1, f32[32]{0:T(128)} %bitcast.2, f32[32]{0:T(128)} %bitcast.3, s32[32]{0:T(128)} %order_hbm.1, s32[32,32]{1,0:T(8,128)} %keep_hbm.1), custom_call_target="tpu_custom_call" | custom-call | tf_op jit(solution)/shard_map/pallas_call | solution.py:400
  46.2 0.8 %shard_map.87 = (bf16[32,8192]{1,0:T(8,128)(2,1)}, f32[32,64]{1,0:T(8,128)}) custom-call(bf16[32,8192]{1,0:T(8,128)(2,1)S(1)} %get-tuple-element.4.rows_in, f32[32,64]{1,0:T(8,128)S(1)} %get-tuple-element.5.checks_in), custom_call_target="tpu_custom_call" | custom-call | tf_op jit(solution)/shard_map/pallas_call | solution.py:444

commit v6 on v5

--- a/solution.py
+++ b/solution.py
@@ -1,3 +1,4 @@
+import itertools
 import math
 
 import jax
@@ -194,9 +195,9 @@
     y_copy(0, 1, 0).wait_recv()
     c_copy(3, 0).start()
     x_copy(0).wait_recv()
-    d_copy(0).start()
     y_copy(1, 0, 0).start()
     y_copy(1, 1, 0).start()
+    d_copy(0).start()
     c_copy(6, 0).start()
     y_copy(0, 1, 1).wait_recv()
     f_copy(1).start()
@@ -204,9 +205,9 @@
     y_copy(0, 0, 1).wait_recv()
     c_copy(2, 1).start()
     x_copy(1).wait_recv()
-    d_copy(1).start()
     y_copy(1, 1, 1).start()
     y_copy(1, 0, 1).start()
+    d_copy(1).start()
     c_copy(6, 1).start()
     run(turn_unit(2, 3))
     from_sibling(0)
@@ -313,13 +314,15 @@
         queries_here(after)
         run(value_unit(0, slot_of(step), even), score_unit(0, after, odd), *more)
 
+    def send(slot):
+        finish(slot, False)
+        for copy in out_copy(slot):
+            copy.start()
+
     def second(step, even, odd):
         slot = slot_of(step)
         run(value_unit(1, slot, even), score_unit(1, slot_of(step - 1), odd))
-        finish(slot, False)
-        copies = out_copy(slot)
-        copies[0].start()
-        copies[1].start()
+        send(slot)
 
     run(score_unit(0, 0, scores_a), turn_unit(1))
 
@@ -354,17 +357,22 @@
     lax.fori_loop(0, 3, first_pair, 0)
     from_sibling(2, 3, 6)
     first(6, scores_a, scores_b, turn_unit(4, 5, 6, 7))
-    from_sibling(8, 10, 12, 14)
-    run(value_unit(0, slot_of(7), scores_b), score_unit(1, slot_of(7), scores_a),
-        turn_unit(*range(8, CTX)))
+    from_sibling(8)
+    scoring = score_unit(1, slot_of(7), scores_a)
+    run(value_unit(0, slot_of(7), scores_b), itertools.islice(scoring, 3), turn_unit(8, 9))
+    from_sibling(10, 12, 14)
+    run(scoring, turn_unit(*range(10, CTX)))
+
+    run(value_unit(1, slot_of(7), scores_a))
+    send(slot_of(7))
+    run(score_unit(1, slot_of(6), scores_b))
 
     def second_pair(pair, carry):
-        second(7 - 2 * pair, scores_a, scores_b)
         second(6 - 2 * pair, scores_b, scores_a)
+        second(5 - 2 * pair, scores_a, scores_b)
         return carry
 
     lax.fori_loop(0, 3, second_pair, 0)
-    second(1, scores_a, scores_b)
     run(value_unit(1, 0, scores_b))
     finish(0, True)
 

time: 47.1 us -> 46.8 us (level)
  no operation moved by 1% of the time
where the time goes in v6:
time: 46.8 us; the launch traced here: 46.7 us
  Pallas kernels  46 us (98%)
  between operations  0.64 us (1%)
    pallas_call x1, Pallas kernels, local(): pl.pallas_call(kernel, out_shape=(jax.ShapeDtypeStruct((PIECE, 8192), jnp...  45.2 us

profile of v6, /device:TPU:1, one launch (start us, length us, event | category | flops | bytes accessed | tf_op | source)
XLA Modules:
  0.0 46.7 jit_solution(11293022005713273036)
XLA Ops:
  0.6 45.2 %shard_map.86 = (bf16[32,8192]{1,0:T(8,128)(2,1)S(1)}, f32[32,64]{1,0:T(8,128)S(1)}) custom-call(bf16[32,8192]{1,0:T(8,128)(2,1)} %q_hbm.1, bf16[32,1024]{1,0:T(8,128)(2,1)} %k_hbm.1, bf16[32,1024]{1,0:T(8,128)(2,1)} %v_hbm.1, f32[32]{0:T(128)} %bitcast.2, f32[32]{0:T(128)} %bitcast.3, s32[32]{0:T(128)} %order_hbm.1, s32[32,32]{1,0:T(8,128)} %keep_hbm.1), custom_call_target="tpu_custom_call" | custom-call | tf_op jit(solution)/shard_map/pallas_call | solution.py:408
  45.9 0.8 %shard_map.87 = (bf16[32,8192]{1,0:T(8,128)(2,1)}, f32[32,64]{1,0:T(8,128)}) custom-call(bf16[32,8192]{1,0:T(8,128)(2,1)S(1)} %get-tuple-element.4.rows_in, f32[32,64]{1,0:T(8,128)S(1)} %get-tuple-element.5.checks_in), custom_call_target="tpu_custom_call" | custom-call | tf_op jit(solution)/shard_map/pallas_call | solution.py:452

commit v7 on v6

--- a/solution.py
+++ b/solution.py
@@ -29,7 +29,7 @@
     q_hbm, k_hbm, v_hbm, ks_hbm, vs_hbm, order_hbm, keep_hbm,
     out_ref, chk_out,
     ks_ref, vs_ref, order_ref, keep_ref, bias_ref, factor_ref, vfactor_ref,
-    qbuf, kbuf, vbuf, vt, scores_a, scores_b, total, peaks, ostage, cstage, crecv,
+    q_in, k_in, v_in, qbuf, kbuf, vbuf, vt, scores_a, scores_b, total, peaks, ostage, cstage, crecv,
     tab_sem, loc_sem, kv_send, kv_recv, q_send, q_recv, g_send, x_recv, y_recv, f_recv, c_recv, d_recv,
     o_send, o_recv,
 ):
@@ -74,22 +74,29 @@
         )
     ]
     landing = pl.ds(pl.multiple_of(me * PIECE, PIECE), PIECE)
-    own_k = pltpu.make_async_copy(k_hbm.at[:, columns_of(me, 128)], kbuf.at[landing], loc_sem.at[0])
-    own_v = pltpu.make_async_copy(v_hbm.at[:, columns_of(me, 128)], vbuf.at[landing], loc_sem.at[1])
-    own_q = pltpu.make_async_copy(q_hbm.at[:, columns_of(me, 1024)], qbuf.at[0], loc_sem.at[2])
-    for copy in tables + [own_k, own_v, own_q]:
+    staged = [
+        pltpu.make_async_copy(source, target, loc_sem.at[3 + i])
+        for i, (source, target) in enumerate(((k_hbm, k_in), (v_hbm, v_in), (q_hbm, q_in)))
+    ]
+    for copy in staged + tables:
         copy.start()
+    own_k = pltpu.make_async_copy(k_in.at[:, columns_of(me, 128)], kbuf.at[landing], loc_sem.at[0])
+    own_v = pltpu.make_async_copy(v_in.at[:, columns_of(me, 128)], vbuf.at[landing], loc_sem.at[1])
+    own_q = pltpu.make_async_copy(q_in.at[:, columns_of(me, 1024)], qbuf.at[0], loc_sem.at[2])
+    for copy, own in zip(staged, (own_k, own_v, own_q)):
+        copy.wait()
+        own.start()
     pl.semaphore_wait(barrier, HEADS - 1 + 5)
 
     order = [1, 7, 2, 6, 3, 5, 4]
     k_copies, v_copies, q_copies = {}, {}, {}
     for d in range(1, HEADS):
         to = lax.rem(me + d, HEADS)
-        k_copies[d] = remote(k_hbm.at[:, columns_of(to, 128)], kbuf.at[landing],
+        k_copies[d] = remote(k_in.at[:, columns_of(to, 128)], kbuf.at[landing],
                              kv_send.at[0], kv_recv.at[0], peer(d))
-        v_copies[d] = remote(v_hbm.at[:, columns_of(to, 128)], vbuf.at[landing],
+        v_copies[d] = remote(v_in.at[:, columns_of(to, 128)], vbuf.at[landing],
                              kv_send.at[1], kv_recv.at[1], peer(d))
-        q_copies[d] = remote(q_hbm.at[:, columns_of(to, 1024)], qbuf.at[d],
+        q_copies[d] = remote(q_in.at[:, columns_of(to, 1024)], qbuf.at[d],
                              q_send, q_recv.at[d], peer(d))
     for d in reversed(order):
         k_copies[d].start()
@@ -421,6 +428,9 @@
             pltpu.SMEM((2, 32), jnp.float32),
             pltpu.SMEM((32,), jnp.float32),
             pltpu.SMEM((32,), jnp.float32),
+            pltpu.VMEM((PIECE, 8192), jnp.bfloat16),
+            pltpu.VMEM((PIECE, 1024), jnp.bfloat16),
+            pltpu.VMEM((PIECE, 1024), jnp.bfloat16),
             pltpu.VMEM((HEADS, PIECE, 1024), jnp.bfloat16),
             pltpu.VMEM((KEYS, HEAD_WIDTH), jnp.bfloat16),
             pltpu.VMEM((KEYS, HEAD_WIDTH), jnp.bfloat16),
@@ -433,7 +443,7 @@
             pltpu.VMEM((HEADS, HEADS, 128), jnp.float32),
             pltpu.VMEM((HEADS, HEADS, 128), jnp.float32),
             dma((4,)),
-            dma((3,)),
+            dma((6,)),
             dma((2,)), dma((2,)),
             dma, dma((HEADS,)),
             dma((2,)), dma((2,)), dma((2, 2, 2)), dma((2,)), dma((8, 2)), dma((2,)),

time: 46.8 us -> 46.7 us (level)
  no operation moved by 1% of the time
where the time goes in v7:
time: 46.7 us; the launch traced here: 46.6 us
  Pallas kernels  46 us (99%)
  between operations  0.64 us (1%)
    pallas_call x1, Pallas kernels, local(): pl.pallas_call(kernel, out_shape=(jax.ShapeDtypeStruct((PIECE, 8192), jnp...  45.2 us

profile of v7, /device:TPU:1, one launch (start us, length us, event | category | flops | bytes accessed | tf_op | source)
XLA Modules:
  0.0 46.6 jit_solution(2252970445504206643)
XLA Ops:
  0.6 45.2 %shard_map.86 = (bf16[32,8192]{1,0:T(8,128)(2,1)S(1)}, f32[32,64]{1,0:T(8,128)S(1)}) custom-call(bf16[32,8192]{1,0:T(8,128)(2,1)} %q_hbm.1, bf16[32,1024]{1,0:T(8,128)(2,1)} %k_hbm.1, bf16[32,1024]{1,0:T(8,128)(2,1)} %v_hbm.1, f32[32]{0:T(128)} %bitcast.2, f32[32]{0:T(128)} %bitcast.3, s32[32]{0:T(128)} %order_hbm.1, s32[32,32]{1,0:T(8,128)} %keep_hbm.1), custom_call_target="tpu_custom_call" | custom-call | tf_op jit(solution)/shard_map/pallas_call | solution.py:415
  45.8 0.8 %shard_map.87 = (bf16[32,8192]{1,0:T(8,128)(2,1)}, f32[32,64]{1,0:T(8,128)}) custom-call(bf16[32,8192]{1,0:T(8,128)(2,1)S(1)} %get-tuple-element.4.rows_in, f32[32,64]{1,0:T(8,128)S(1)} %get-tuple-element.5.checks_in), custom_call_target="tpu_custom_call" | custom-call | tf_op jit(solution)/shard_map/pallas_call | solution.py:462
